TPU v7x, 32 devices: a whole 2x2x4 slice. The times are simulated.
32 devices in a mesh: batch: 4 (over z), seq: 8 (over y, x, core).
Axes of the slice: x: 2, y: 2, z: 4, core: 2. Of those that a mesh axis runs over, the one named last changes fastest.
Arguments:
- inputs: bfloat16 [2, 4, 4096, 768], P(None, 'batch', 'seq'), may hold values from -6 to 6
- cotangent: bfloat16 [2, 4, 4096, 768], P(None, 'batch', 'seq'), may hold values from -6 to 6
- pre_gain: bfloat16 [768], P(('batch', 'seq')), may hold values from 0.099609375 to 1.8984375
- qkv_weight: bfloat16 [768, 2304], P(('batch', 'seq')), may hold values from -0.21875 to 0.21875
- qv_bias: bfloat16 [1536], P(('batch', 'seq')), may hold values from -3 to 3
- mid_gain: bfloat16 [768], P(('batch', 'seq')), may hold values from 0.099609375 to 1.8984375
- out_weight: bfloat16 [768, 768], P(('batch', 'seq')), may hold values from -0.21875 to 0.21875
- out_bias: bfloat16 [768], P(('batch', 'seq')), may hold values from -3 to 3
- ffn_gain: bfloat16 [768], P(('batch', 'seq')), may hold values from 0.099609375 to 1.8984375
- up_weight: bfloat16 [768, 3072], P(('batch', 'seq')), may hold values from -0.21875 to 0.21875
- up_bias: bfloat16 [3072], P(('batch', 'seq')), may hold values from -3 to 3
- sub_gain: bfloat16 [3072], P(('batch', 'seq')), may hold values from 0.099609375 to 1.8984375
- down_weight: bfloat16 [3072, 768], P(('batch', 'seq')), may hold values from -0.109375 to 0.109375
- down_bias: bfloat16 [768], P(('batch', 'seq')), may hold values from -3 to 3
- pic_starts: int32 [2, 4, 4], P(None, 'batch'), may hold values from 0 to 3840, as said below
- head_offsets: int32 [12], replicated, may hold values from 0 to 1
Outputs:
- layer_out: bfloat16 [2, 4, 4096, 768], P(None, 'batch', 'seq')
- input_grad: bfloat16 [2, 4, 4096, 768], P(None, 'batch', 'seq')
- pregain_grad: float32 [768], P(('batch', 'seq'))
- qkv_grad: float32 [768, 2304], P(('batch', 'seq'))
- qvbias_grad: float32 [1536], P(('batch', 'seq'))
- midgain_grad: float32 [768], P(('batch', 'seq'))
- outweight_grad: float32 [768, 768], P(('batch', 'seq'))
- outbias_grad: float32 [768], P(('batch', 'seq'))
- ffngain_grad: float32 [768], P(('batch', 'seq'))
- upweight_grad: float32 [768, 3072], P(('batch', 'seq'))
- upbias_grad: float32 [3072], P(('batch', 'seq'))
- subgain_grad: float32 [3072], P(('batch', 'seq'))
- downweight_grad: float32 [3072, 768], P(('batch', 'seq'))
- downbias_grad: float32 [768], P(('batch', 'seq'))
Inputs may be any that keep to these rules, and one draw needn't show every extreme that they name: `pic_starts`: piece n of a sequence starts at n * 1024 or later and ends by (n + 1) * 1024, so pieces never intersect.
All inputs are finite; a program needn't handle non-finite values.
Results may differ from a plain program's by a relative error of at most 0.019.
Values may be sent and summed in bfloat16 or wider, within the bound.
No kernel may reach another device: no remote copies, remote signals or barrier semaphores. Data moves between devices by JAX's collectives and lax.ppermute only.
A program may use at most 384 MiB of HBM per device.

v0:
```python
from functools import partial
import math

import jax
import jax.numpy as jnp
from jax import lax
from jax.sharding import PartitionSpec as P

HEADS = 12
HD = 64
SEG_SHORT = 2048
SEG_LONG = 4096
PIC = 256


def layer_norm(values, gain):
    centred = values - jnp.mean(values, axis=-1, keepdims=True)
    spread = jnp.mean(centred * centred, axis=-1, keepdims=True)
    return centred * lax.rsqrt(spread + 1e-05) * gain


def piece_table(positions, starts):
    inside = (positions[None, :, None] >= starts[:, None, :]) & (
        positions[None, :, None] < starts[:, None, :] + PIC
    )
    labels = jnp.arange(1, starts.shape[1] + 1, dtype=jnp.int32)
    return jnp.sum(jnp.where(inside, labels, 0), axis=-1)


def counts_from(query_pos, key_pos, query_piece, key_piece, offsets):
    shared = (key_piece.T[:, :, None] == query_piece[None, :, :]) & (query_piece[None, :, :] > 0)
    causal = (key_pos[:, None] <= query_pos[None, :])[:, None, :]
    allowed = shared | causal
    key_col = key_pos[:, None]
    query_row = query_pos[None, :]
    near_segment = (key_col // SEG_SHORT == query_row // SEG_SHORT)[:, None, :]
    far_segment = ((key_col // SEG_LONG == query_row // SEG_LONG) & (key_col % 2 == query_row % 2))[
        :, None, :
    ]
    active = query_row % 2 == offsets[:, None]
    first_count = (allowed & near_segment).astype(jnp.float32)[:, :, None, :]
    second = ((allowed & far_segment)[:, :, None, :] & active[None, None, :, :]).astype(jnp.float32)
    return first_count + second


def block_size(length, local_rows, sequences):
    wanted = max(1, 512 // (local_rows * sequences))
    return local_rows * math.gcd(length // local_rows, wanted)


def key_limit(query_pos, starts):
    first_row = query_pos[0]
    last_row = query_pos[-1]
    ends = starts + PIC
    intersection = (starts <= last_row) & (ends > first_row)
    return jnp.maximum(last_row + 1, jnp.max(jnp.where(intersection, ends, 0)))


def key_piece_at(gathered, whole_pieces, number, key_block, sequences):
    key_piece = lax.dynamic_slice_in_dim(gathered, number * key_block, key_block, 1)
    model_width = key_piece.shape[2] // 2
    key_rows = key_piece[..., :model_width].reshape(sequences, key_block, HEADS, HD)
    values = key_piece[..., model_width:].reshape(sequences, key_block, HEADS, HD)
    key_pos = number * key_block + jnp.arange(key_block, dtype=jnp.int32)
    labels = lax.dynamic_slice_in_dim(whole_pieces, number * key_block, key_block, 1)
    return (key_rows, values, key_pos, labels)


def attend_forward(
    queries, gathered, query_pos, query_piece, whole_pieces, limit, offsets, key_block, score_scale
):
    sequences, local_rows = (queries.shape[0], queries.shape[1])
    blocks = gathered.shape[1] // key_block

    def advance(carry, number):

        def compute(state):
            running_max, running_sum, running_out = state
            key_rows, values, key_pos, labels = key_piece_at(
                gathered, whole_pieces, number, key_block, sequences
            )
            scores = (
                jnp.einsum("sqhe,skhe->kshq", queries, key_rows, preferred_element_type=jnp.float32)
                * score_scale
            )
            counts = counts_from(query_pos, key_pos, query_piece, labels, offsets)
            new_max = jnp.maximum(
                running_max, jnp.max(jnp.where(counts > 0, scores, -1e30), axis=0)
            )
            factor = jnp.exp(running_max - new_max)
            weights = counts * jnp.exp(jnp.where(counts > 0, scores - new_max, -1e30))
            running_sum = running_sum * factor + jnp.sum(weights, axis=0)
            product = jnp.einsum(
                "kshq,skhe->sqhe",
                weights.astype(jnp.bfloat16),
                values,
                preferred_element_type=jnp.float32,
            )
            running_out = running_out * jnp.transpose(factor, (0, 2, 1))[..., None] + product
            return (new_max, running_sum, running_out)

        return (lax.cond(number * key_block < limit, compute, lambda state: state, carry), None)

    initial = (
        jnp.full((sequences, HEADS, local_rows), -1e30, jnp.float32),
        jnp.zeros((sequences, HEADS, local_rows), jnp.float32),
        jnp.zeros((sequences, local_rows, HEADS, HD), jnp.float32),
    )
    (running_max, running_sum, running_out), _ = lax.scan(advance, initial, jnp.arange(blocks))
    attended = running_out / jnp.transpose(running_sum, (0, 2, 1))[..., None]
    return (attended, running_max + jnp.log(running_sum))


def attend_backward(
    queries,
    gathered,
    grad_heads,
    log_total,
    row_dots,
    query_pos,
    query_piece,
    whole_pieces,
    limit,
    offsets,
    key_block,
):
    sequences, local_rows = (queries.shape[0], queries.shape[1])
    blocks = gathered.shape[1] // key_block
    model_width = gathered.shape[2] // 2
    score_scale = 1.0 / math.sqrt(HD)
    term_shape = (key_block, sequences, 2 * model_width)

    def advance(running_grad, number):

        def compute(total):
            key_rows, values, key_pos, labels = key_piece_at(
                gathered, whole_pieces, number, key_block, sequences
            )
            scores = (
                jnp.einsum("sqhe,skhe->kshq", queries, key_rows, preferred_element_type=jnp.float32)
                * score_scale
            )
            counts = counts_from(query_pos, key_pos, query_piece, labels, offsets)
            probs_exact = counts * jnp.exp(jnp.where(counts > 0, scores - log_total, -1e30))
            slopes_in = jnp.einsum(
                "sqhe,skhe->kshq", grad_heads, values, preferred_element_type=jnp.float32
            )
            slopes = (probs_exact * (slopes_in - row_dots)).astype(jnp.bfloat16)
            total = total + jnp.einsum(
                "kshq,skhe->sqhe", slopes, key_rows, preferred_element_type=jnp.float32
            )
            key_part = (
                jnp.einsum("kshq,sqhe->kshe", slopes, queries, preferred_element_type=jnp.float32)
                * score_scale
            )
            value_part = jnp.einsum(
                "kshq,sqhe->kshe",
                probs_exact.astype(jnp.bfloat16),
                grad_heads,
                preferred_element_type=jnp.float32,
            )
            term = jnp.concatenate(
                [
                    key_part.reshape(key_block, sequences, model_width),
                    value_part.reshape(key_block, sequences, model_width),
                ],
                axis=-1,
            )
            return (total, term.astype(jnp.bfloat16))

        def skip(total):
            return (total, jnp.zeros(term_shape, jnp.bfloat16))

        return lax.cond(number * key_block < limit, compute, skip, running_grad)

    initial = jnp.zeros((sequences, local_rows, HEADS, HD), jnp.float32)
    query_grad, terms = lax.scan(advance, initial, jnp.arange(blocks))
    return (
        query_grad * score_scale,
        terms.reshape((blocks * key_block, sequences, 2 * model_width)),
    )


def on_device(
    inputs,
    cotangent,
    pre_gain,
    qkv_weight,
    qv_bias,
    mid_gain,
    out_weight,
    out_bias,
    ffn_gain,
    up_weight,
    up_bias,
    sub_gain,
    down_weight,
    down_bias,
    pic_starts,
    head_offsets,
):
    score_scale = 1.0 / math.sqrt(HD)
    sequences = inputs.shape[1]
    local_rows = inputs.shape[2]
    model_width = inputs.shape[3]
    length = local_rows * lax.axis_size("seq")
    key_block = block_size(length, local_rows, sequences)
    query_pos = lax.axis_index("seq") * local_rows + jnp.arange(local_rows, dtype=jnp.int32)
    all_pos = jnp.arange(length, dtype=jnp.int32)
    shard_list = (
        pre_gain,
        qkv_weight,
        qv_bias,
        mid_gain,
        out_weight,
        out_bias,
        ffn_gain,
        up_weight,
        up_bias,
        sub_gain,
        down_weight,
        down_bias,
    )
    copies = lax.axis_size("batch") * lax.axis_size("seq")
    totals = [
        jnp.zeros((item.shape[0] * copies,) + item.shape[1:], jnp.float32) for item in shard_list
    ]

    def fetch_params():
        return (
            lax.all_gather(pre_gain, ("batch", "seq"), axis=0, tiled=True),
            lax.all_gather(qkv_weight, ("batch", "seq"), axis=0, tiled=True),
            lax.all_gather(qv_bias, ("batch", "seq"), axis=0, tiled=True),
            lax.all_gather(mid_gain, ("batch", "seq"), axis=0, tiled=True),
            lax.all_gather(out_weight, ("batch", "seq"), axis=0, tiled=True),
            lax.all_gather(out_bias, ("batch", "seq"), axis=0, tiled=True),
            lax.all_gather(ffn_gain, ("batch", "seq"), axis=0, tiled=True),
            lax.all_gather(up_weight, ("batch", "seq"), axis=0, tiled=True),
            lax.all_gather(up_bias, ("batch", "seq"), axis=0, tiled=True),
            lax.all_gather(sub_gain, ("batch", "seq"), axis=0, tiled=True),
            lax.all_gather(down_weight, ("batch", "seq"), axis=0, tiled=True),
            lax.all_gather(down_bias, ("batch", "seq"), axis=0, tiled=True),
        )

    results = []
    input_grads = []
    gelu_exact = partial(jax.nn.gelu, approximate=False)
    for micro_index in range(inputs.shape[0]):
        params = fetch_params()
        (
            gain_pre,
            weight_qkv,
            bias_qv,
            gain_mid,
            weight_out,
            bias_out,
            gain_ffn,
            weight_up,
            bias_up,
            gain_sub,
            weight_down,
            bias_down,
        ) = params
        starts = pic_starts[micro_index]
        whole_pieces = piece_table(all_pos, starts)
        query_piece = piece_table(query_pos, starts)
        limit = key_limit(query_pos, starts)
        tokens_in = inputs[micro_index].astype(jnp.float32)
        normed = layer_norm(tokens_in, gain_pre.astype(jnp.float32))
        normed_low = normed.astype(jnp.bfloat16)
        bias_full = jnp.concatenate(
            [bias_qv[:model_width], jnp.zeros((model_width,), jnp.bfloat16), bias_qv[model_width:]]
        ).astype(jnp.float32)
        projected = (
            jnp.dot(normed_low, weight_qkv, preferred_element_type=jnp.float32) + bias_full
        ).astype(jnp.bfloat16)
        queries = projected[..., :model_width].reshape(sequences, local_rows, HEADS, HD)
        key_values = projected[..., model_width:]
        gathered = lax.all_gather(key_values, "seq", axis=1, tiled=True)
        attended, log_total = attend_forward(
            queries,
            gathered,
            query_pos,
            query_piece,
            whole_pieces,
            limit,
            head_offsets,
            key_block,
            score_scale,
        )
        attn_flat = attended.reshape(sequences, local_rows, model_width)
        mid_low = layer_norm(attn_flat, gain_mid.astype(jnp.float32)).astype(jnp.bfloat16)
        middle = (
            tokens_in
            + jnp.dot(mid_low, weight_out, preferred_element_type=jnp.float32)
            + bias_out.astype(jnp.float32)
        )
        ffn_low = layer_norm(middle, gain_ffn.astype(jnp.float32)).astype(jnp.bfloat16)
        before = jnp.dot(ffn_low, weight_up, preferred_element_type=jnp.float32) + bias_up.astype(
            jnp.float32
        )
        activated = gelu_exact(before)
        sub_low = layer_norm(activated, gain_sub.astype(jnp.float32)).astype(jnp.bfloat16)
        finished = (
            middle
            + jnp.dot(sub_low, weight_down, preferred_element_type=jnp.float32)
            + bias_down.astype(jnp.float32)
        )
        results.append(finished.astype(jnp.bfloat16))
        params = fetch_params()
        (
            gain_pre,
            weight_qkv,
            bias_qv,
            gain_mid,
            weight_out,
            bias_out,
            gain_ffn,
            weight_up,
            bias_up,
            gain_sub,
            weight_down,
            bias_down,
        ) = params
        upstream = cotangent[micro_index].astype(jnp.float32)
        down_grad = upstream.astype(jnp.bfloat16)
        grad_downw = jnp.einsum(
            "sqf,sqd->fd", sub_low, down_grad, preferred_element_type=jnp.float32
        )
        grad_downb = jnp.sum(down_grad.astype(jnp.float32), axis=(0, 1))
        sub_grad = jnp.einsum(
            "sqd,fd->sqf", down_grad, weight_down, preferred_element_type=jnp.float32
        )
        _, sub_back = jax.vjp(layer_norm, activated, gain_sub.astype(jnp.float32))
        act_grad, grad_subgain = sub_back(sub_grad)
        _, gelu_back = jax.vjp(gelu_exact, before)
        before_grad = gelu_back(act_grad)[0].astype(jnp.bfloat16)
        grad_upw = jnp.einsum(
            "sqd,sqf->df", ffn_low, before_grad, preferred_element_type=jnp.float32
        )
        grad_upb = jnp.sum(before_grad.astype(jnp.float32), axis=(0, 1))
        ffn_grad = jnp.einsum(
            "sqf,df->sqd", before_grad, weight_up, preferred_element_type=jnp.float32
        )
        _, ffn_back = jax.vjp(layer_norm, middle, gain_ffn.astype(jnp.float32))
        middle_part, grad_ffngain = ffn_back(ffn_grad)
        middle_grad = upstream + middle_part
        branch_grad = middle_grad.astype(jnp.bfloat16)
        grad_outw = jnp.einsum(
            "sqd,sqe->de", mid_low, branch_grad, preferred_element_type=jnp.float32
        )
        grad_outb = jnp.sum(branch_grad.astype(jnp.float32), axis=(0, 1))
        mid_grad = jnp.einsum(
            "sqe,de->sqd", branch_grad, weight_out, preferred_element_type=jnp.float32
        )
        _, mid_back = jax.vjp(layer_norm, attn_flat, gain_mid.astype(jnp.float32))
        attn_grad, grad_midgain = mid_back(mid_grad)
        grad_heads = attn_grad.astype(jnp.bfloat16).reshape(sequences, local_rows, HEADS, HD)
        dots_rows = jnp.sum(grad_heads.astype(jnp.float32) * attended, axis=-1)
        row_dots = jnp.transpose(dots_rows, (0, 2, 1))
        gathered = lax.all_gather(key_values, "seq", axis=1, tiled=True)
        query_grad, term_store = attend_backward(
            queries,
            gathered,
            grad_heads,
            log_total,
            row_dots,
            query_pos,
            query_piece,
            whole_pieces,
            limit,
            head_offsets,
            key_block,
        )
        pair_grad = lax.psum_scatter(
            term_store.astype(jnp.float32).astype(jnp.bfloat16),
            "seq",
            scatter_dimension=0,
            tiled=True,
        ).astype(jnp.float32)
        pair_low = jnp.transpose(pair_grad, (1, 0, 2)).astype(jnp.bfloat16)
        query_low = query_grad.reshape(sequences, local_rows, model_width).astype(jnp.bfloat16)
        proj_grad = jnp.concatenate([query_low, pair_low], axis=-1)
        grad_qkvw = jnp.einsum(
            "sqd,sqf->df", normed_low, proj_grad, preferred_element_type=jnp.float32
        )
        grad_qvb = jnp.concatenate(
            [
                jnp.sum(query_low.astype(jnp.float32), axis=(0, 1)),
                jnp.sum(pair_low[..., model_width:].astype(jnp.float32), axis=(0, 1)),
            ]
        )
        normed_grad = jnp.einsum(
            "sqf,df->sqd", proj_grad, weight_qkv, preferred_element_type=jnp.float32
        )
        _, pre_back = jax.vjp(layer_norm, tokens_in, gain_pre.astype(jnp.float32))
        input_part, grad_pregain = pre_back(normed_grad)
        input_grads.append((middle_grad + input_part).astype(jnp.bfloat16))
        updates = (
            grad_pregain,
            grad_qkvw,
            grad_qvb,
            grad_midgain,
            grad_outw,
            grad_outb,
            grad_ffngain,
            grad_upw,
            grad_upb,
            grad_subgain,
            grad_downw,
            grad_downb,
        )
        totals = [running + update for running, update in zip(totals, updates)]
    owned_grads = (
        lax.psum_scatter(totals[0], ("batch", "seq"), scatter_dimension=0, tiled=True),
        lax.psum_scatter(totals[1], ("batch", "seq"), scatter_dimension=0, tiled=True),
        lax.psum_scatter(totals[2], ("batch", "seq"), scatter_dimension=0, tiled=True),
        lax.psum_scatter(totals[3], ("batch", "seq"), scatter_dimension=0, tiled=True),
        lax.psum_scatter(totals[4], ("batch", "seq"), scatter_dimension=0, tiled=True),
        lax.psum_scatter(totals[5], ("batch", "seq"), scatter_dimension=0, tiled=True),
        lax.psum_scatter(totals[6], ("batch", "seq"), scatter_dimension=0, tiled=True),
        lax.psum_scatter(totals[7], ("batch", "seq"), scatter_dimension=0, tiled=True),
        lax.psum_scatter(totals[8], ("batch", "seq"), scatter_dimension=0, tiled=True),
        lax.psum_scatter(totals[9], ("batch", "seq"), scatter_dimension=0, tiled=True),
        lax.psum_scatter(totals[10], ("batch", "seq"), scatter_dimension=0, tiled=True),
        lax.psum_scatter(totals[11], ("batch", "seq"), scatter_dimension=0, tiled=True),
    )
    return (jnp.stack(results), jnp.stack(input_grads)) + tuple(owned_grads)


def solution(mesh):
    placed = (
        P(None, "batch", "seq", None),
        P(None, "batch", "seq", None),
        P(("batch", "seq")),
        P(("batch", "seq"), None),
        P(("batch", "seq")),
        P(("batch", "seq")),
        P(("batch", "seq"), None),
        P(("batch", "seq")),
        P(("batch", "seq")),
        P(("batch", "seq"), None),
        P(("batch", "seq")),
        P(("batch", "seq")),
        P(("batch", "seq"), None),
        P(("batch", "seq")),
        P(None, "batch", None),
        P(),
    )
    return jax.shard_map(
        on_device,
        mesh=mesh,
        in_specs=placed,
        out_specs=(
            P(None, "batch", "seq", None),
            P(None, "batch", "seq", None),
            P(("batch", "seq")),
            P(("batch", "seq"), None),
            P(("batch", "seq")),
            P(("batch", "seq")),
            P(("batch", "seq"), None),
            P(("batch", "seq")),
            P(("batch", "seq")),
            P(("batch", "seq"), None),
            P(("batch", "seq")),
            P(("batch", "seq")),
            P(("batch", "seq"), None),
            P(("batch", "seq")),
        ),
        check_vma=False,
    )
```

profile of v0, /device:TPU:0, one launch (start us, length us, event | category | flops | bytes accessed | tf_op | source)
XLA Modules:
  0.0 1779.7 jit_solution(2114318883928608655)
XLA Ops:
  14.7 42.9 %all-reduce.17 = (bf16[768]{0:T(1024)(128)(2,1)S(1)}, bf16[1536]{0:T(1024)(128)(2,1)S(1)}, bf16[768]{0:T(1024)(128)(2,1)S(1)}, bf16[768]{0:T(1024)(128)(2,1)S(1)...) all-reduce(bf16[768]{0:T(1024)(128)(2,1)S(1)} %dynamic-update-slice, ...), channel_id=1, replica_groups=mesh['batch'=4,'seq'=8] {'batch','seq'}, use_global_device_ids=true, to_apply=%add.3 | all-reduce | flops 11520 | bytes 46080
  62.0 11.8 all-gather.7.cloned.1.call-done
  99.7 52.0 %all-gather.9.cloned.1.call-done = bf16[1,4096,1536]{2,1,0:T(8,128)(2,1)} async-done(((bf16[1,512,1536]{2,1,0:T(8,128)(2,1)}), bf16[1,4096,1536]{2,1,0:T(8,128)(2,1)}) %all-gather.9.cloned.1.call-update) | async-done | bytes 12582928 | tf_op jit(solution)/shard_map/all_gather | solution.py:279
  151.7 16.9 copy.89
  168.8 27.9 %while.62 = (s32[]{:T(128)}, f32[1,12,512]{2,1,0:T(8,128)S(1)}, f32[1,12,512]{2,1,0:T(8,128)S(1)}, f32[1,512,12,64]{1,3,2,0:T(8,128)S(1)}, s32[8]{0:T(128)S(1)},...) while((s32[]{:T(128)}, f32[1,12,512]{2,1,0:T(8,128)S(1)}, ...), condition=%wide.region_10.11_spmd.clone, body=%wide.region_5.10_spmd.clone.sunk | while | flops 887685120 | bytes 52112832 | solution.py:109
  170.1 17.6 conditional.12
  196.8 29.5 %all-gather.17.cloned.1.call-done = bf16[1,4096,1536]{2,1,0:T(8,128)(2,1)} async-done(((bf16[1,512,1536]{2,1,0:T(8,128)(2,1)}), bf16[1,4096,1536]{2,1,0:T(8,128)(2,1)}) %all-gather.17.cloned.1.call-update) | async-done | bytes 12582928 | tf_op jit(solution)/shard_map/all_gather | solution.py:279
  226.3 16.1 copy.92
  242.7 46.0 %while.63 = (s32[]{:T(128)}, f32[1,12,512]{2,1,0:T(8,128)S(1)}, f32[1,12,512]{2,1,0:T(8,128)S(1)}, f32[1,512,12,64]{1,3,2,0:T(8,128)S(1)}, s32[8]{0:T(128)S(1)},...) while((s32[]{:T(128)}, f32[1,12,512]{2,1,0:T(8,128)S(1)}, ...), condition=%wide.region_27.28_spmd.clone, body=%wide.region_22.27_spmd.clone.sunk | while | flops 887685120 | bytes 52112832 | solution.py:109
  244.5 17.6 conditional.13
  263.3 17.6 conditional.13
  307.5 41.0 %all-gather.13.cloned.1.call-done = bf16[768,3072]{1,0:T(8,128)(2,1)} async-done(((bf16[24,3072]{1,0:T(8,128)(2,1)}), bf16[768,3072]{1,0:T(8,128)(2,1)}) %all-gather.13.cloned.1.call-update) | async-done | bytes 4718608 | tf_op jit(solution)/shard_map/all_gather | solution.py:238
  353.8 33.4 %fusion.238 = (f32[512]{0:T(512)S(1)}, f32[512,3072]{1,0:T(8,128)}, f32[512,3072]{1,0:T(8,128)}, f32[512]{0:T(512)S(1)}, f32[512,3072]{1,0:T(8,128)}, /*index=5*/f32[512,3072]{1,0:T(8,128)}, f32[512,3072]{1,0:T(8,128)}) fusion(f32[3072]{0:T(1024)S(1)} %copy-done.88, f32[512,3072]{1,0:T(8,128)S(1)} %fusion.229, bf16[768,3072]{1,0:T(8,128)(2,1)S(1)} %copy-done.127, ...), kind=kOutput, calls=%fused_computation.515 | convolution fusion | flops 2625108992 | bytes 44063744 | tf_op jit(solution)/shard_map/dot_general | solution.py:299
  387.2 26.5 %all-gather.15.cloned.1.call-done = bf16[3072,768]{1,0:T(8,128)(2,1)} async-done(((bf16[96,768]{1,0:T(8,128)(2,1)}), bf16[3072,768]{1,0:T(8,128)(2,1)}) %all-gather.15.cloned.1.call-update) | async-done | bytes 4718608 | tf_op jit(solution)/shard_map/all_gather | solution.py:241
  422.0 11.2 multiply_reduce_fusion.1
  436.6 16.5 convert_reduce_fusion.1
  479.5 57.9 %while.64 = (s32[]{:T(128)}, f32[1,512,12,64]{1,3,2,0:T(8,128)}, bf16[8,512,1,1536]{3,1,0,2:T(8,128)(2,1)}, s32[8]{0:T(128)S(1)}, s32[]{:T(128)}, /*index=5*/bf1...) while((s32[]{:T(128)}, f32[1,512,12,64]{1,3,2,0:T(8,128)}, ...), condition=%wide.region_44.45_spmd.clone, body=%wide.region_41.44_spmd.clone.sunk | while | flops 2083829760 | bytes 146421328 | solution.py:177
  480.9 29.3 %conditional.14 = (f32[1,512,12,64]{1,3,2,0:T(8,128)}, bf16[1,512,1,1536]{1,3,2,0:T(8,128)(2,1)S(1)}) conditional(s32[]{:T(128)} %convert_element_type.869, f32[1,512,12,64]{1,3,2,0:T(8,128)} %get-tuple-element.1638, (s32[]{:T(128)}, bf16[1,4096,1536]{1,2,0:T(8,128)(2,1)}, s32[1,4096]{1,0:T(1,128)}, s32[1,512]{1,0:T(1,128)S(1)}, s32[]{:T(128)}, ...), branch_computations={%region_42.42_spmd, %region_43.43_spmd} | conditional | flops 2083829760 | bytes 133836008 | solution.py:174
  550.7 89.1 %while.65 = (s32[]{:T(128)}, f32[1,512,12,64]{1,3,2,0:T(8,128)}, bf16[8,512,1,1536]{3,1,0,2:T(8,128)(2,1)}, s32[8]{0:T(128)S(1)}, s32[]{:T(128)}, /*index=5*/bf1...) while((s32[]{:T(128)}, f32[1,512,12,64]{1,3,2,0:T(8,128)}, ...), condition=%wide.region_58.59_spmd.clone, body=%wide.region_55.58_spmd.clone.sunk | while | flops 2083829760 | bytes 133838280 | solution.py:177
  552.1 31.0 %conditional.15 = (f32[1,512,12,64]{1,3,2,0:T(8,128)}, bf16[1,512,1,1536]{1,3,2,0:T(8,128)(2,1)S(1)}) conditional(s32[]{:T(128)} %convert_element_type.870, f32[1,512,12,64]{1,3,2,0:T(8,128)} %get-tuple-element.1590, (s32[]{:T(128)}, bf16[1,4096,1536]{1,2,0:T(8,128)(2,1)}, s32[1,4096]{1,0:T(1,128)}, s32[1,512]{1,0:T(1,128)S(1)}, s32[]{:T(128)}, ...), branch_computations={%region_56.56_spmd, %region_57.57_spmd} | conditional | flops 2083829760 | bytes 127544488 | solution.py:174
  570.2 9.6 fusion.94
  586.3 31.0 %conditional.15 = (f32[1,512,12,64]{1,3,2,0:T(8,128)}, bf16[1,512,1,1536]{1,3,2,0:T(8,128)(2,1)S(1)}) conditional(s32[]{:T(128)} %convert_element_type.870, f32[1,512,12,64]{1,3,2,0:T(8,128)} %get-tuple-element.1590, (s32[]{:T(128)}, bf16[1,4096,1536]{1,2,0:T(8,128)(2,1)}, s32[1,4096]{1,0:T(1,128)}, s32[1,512]{1,0:T(1,128)S(1)}, s32[]{:T(128)}, ...), branch_computations={%region_56.56_spmd, %region_57.57_spmd} | conditional | flops 2083829760 | bytes 127544488 | solution.py:174
  604.4 9.6 fusion.94
  663.0 9.4 convolution_add_fusion.1
  682.5 284.8 %reduce-scatter.7.cloned.1.call-done = bf16[512,1,1536]{2,0,1:T(8,128)(2,1)} async-done(((bf16[4096,1,1536]{2,0,1:T(8,128)(2,1)}), bf16[512,1,1536]{2,0,1:T(8,128)(2,1)}) %reduce-scatter.7.cloned.1.call-update) | async-done | bytes 1572880 | tf_op jit(solution)/shard_map/reduce_scatter | solution.py:375
  974.0 285.5 %reduce-scatter.9.cloned.1.call-done = bf16[512,1,1536]{2,0,1:T(8,128)(2,1)} async-done(((bf16[4096,1,1536]{2,0,1:T(8,128)(2,1)}), bf16[512,1,1536]{2,0,1:T(8,128)(2,1)}) %reduce-scatter.9.cloned.1.call-update) | async-done | bytes 1572880 | tf_op jit(solution)/shard_map/reduce_scatter | solution.py:375
  1259.6 8.8 convolution_add_fusion
  1293.2 40.7 %all-reduce.16 = (f32[768]{0:T(1024)S(1)}, f32[1536]{0:T(1024)S(1)}, f32[768]{0:T(1024)S(1)}, f32[768]{0:T(1024)S(1)}, f32[768]{0:T(1024)S(1)}, /*index=5*/f32[3...) all-reduce(f32[768]{0:T(1024)S(1)} %add.692, ...), channel_id=4, replica_groups=mesh['batch'=4,'seq'=8] {'batch','seq'}, use_global_device_ids=true, to_apply=%region_64.65.clone | all-reduce | flops 11520 | bytes 92160
  1343.5 21.0 %reduce-scatter.13.cloned.1.call-done = f32[24,768]{1,0:T(8,128)} async-done(((f32[768,768]{1,0:T(8,128)}), f32[24,768]{1,0:T(8,128)}) %reduce-scatter.13.cloned.1.call-update) | async-done | bytes 73744 | tf_op jit(solution)/shard_map/reduce_scatter | solution.py:419
  1364.4 141.8 %reduce-scatter.15.cloned.1.call-done = f32[24,3072]{1,0:T(8,128)} async-done(((f32[768,3072]{1,0:T(8,128)}), f32[24,3072]{1,0:T(8,128)}) %reduce-scatter.15.cloned.1.call-update) | async-done | bytes 294928 | tf_op jit(solution)/shard_map/reduce_scatter | solution.py:422
  1506.3 141.1 %reduce-scatter.17.cloned.1.call-done = f32[96,768]{1,0:T(8,128)} async-done(((f32[3072,768]{1,0:T(8,128)}), f32[96,768]{1,0:T(8,128)}) %reduce-scatter.17.cloned.1.call-update) | async-done | bytes 294928 | tf_op jit(solution)/shard_map/reduce_scatter | solution.py:425
  1647.4 125.3 %reduce-scatter.11.cloned.1.call-done = f32[24,2304]{1,0:T(8,128)} async-done(((f32[768,2304]{1,0:T(8,128)}), f32[24,2304]{1,0:T(8,128)}) %reduce-scatter.11.cloned.1.call-update) | async-done | bytes 221200 | tf_op jit(solution)/shard_map/reduce_scatter | solution.py:416
  (696 shorter events, 360.1 us)
Async XLA Ops:
  7.2 66.6 %copy-start.3 = (bf16[2,1,512,768]{3,2,1,0:T(8,128)(2,1)S(1)}, bf16[2,1,512,768]{3,2,1,0:T(8,128)(2,1)}, u32[]{:S(2)}) copy-start(bf16[2,1,512,768]{3,2,1,0:T(8,128)(2,1)} %param.32) | copy-start | bytes 4718596
  7.2 66.6 %all-gather.7.cloned.1.call-start = ((), (), s32[]{:S(2)}) async-start(), calls=%async_computation.6 | async-start | bytes 3649536 | tf_op jit(solution)/shard_map/all_gather | solution.py:232
  7.9 143.8 %all-gather.9.cloned.1.call-start = ((), (), s32[]{:S(2)}) async-start(), calls=%async_computation.7 | async-start | bytes 14155776 | tf_op jit(solution)/shard_map/all_gather | solution.py:279
  80.6 145.7 %all-gather.17.cloned.1.call-start = ((), (), s32[]{:S(2)}) async-start(), calls=%async_computation.11 | async-start | bytes 14155776 | tf_op jit(solution)/shard_map/all_gather | solution.py:279
  87.5 207.8 %all-gather.11.cloned.1.call-start = ((), (), s32[]{:S(2)}) async-start(), calls=%async_computation.8 | async-start | bytes 1216512 | tf_op jit(solution)/shard_map/all_gather | solution.py:235
  88.1 260.4 %all-gather.13.cloned.1.call-start = ((), (), s32[]{:S(2)}) async-start(), calls=%async_computation.9 | async-start | bytes 4866048 | tf_op jit(solution)/shard_map/all_gather | solution.py:238
  88.7 325.1 %all-gather.15.cloned.1.call-start = ((), (), s32[]{:S(2)}) async-start(), calls=%async_computation.10 | async-start | bytes 4866048 | tf_op jit(solution)/shard_map/all_gather | solution.py:241
  89.2 878.1 %reduce-scatter.7.cloned.1.call-start = ((), (), s32[]{:S(2)}) async-start(), calls=%async_computation.12 | async-start | bytes 14155776 | tf_op jit(solution)/shard_map/reduce_scatter | solution.py:375
  99.7 69.1 %copy-start.63 = (s32[12]{0:T(128)S(1)}, s32[12]{0:T(128)}, u32[]{:S(2)}) copy-start(s32[12]{0:T(128)} %param.47) | copy-start | bytes 148
  295.0 173.6 %copy-start.82 = (f32[512]{0:T(512)}, f32[512]{0:T(512)S(1)}, u32[]{:S(2)}) copy-start(f32[512]{0:T(512)S(1)} %broadcast_multiply_fusion.3) | copy-start | bytes 6148
  295.2 173.4 %copy-start.96 = (f32[512]{0:T(512)}, f32[512]{0:T(512)S(1)}, u32[]{:S(2)}) copy-start(f32[512]{0:T(512)S(1)} %fusion.215) | copy-start | bytes 6148
  298.6 162.4 %copy-start.86 = (f32[512]{0:T(512)}, f32[512]{0:T(512)S(1)}, u32[]{:S(2)}) copy-start(f32[512]{0:T(512)S(1)} %broadcast_multiply_fusion.2) | copy-start | bytes 6148
  300.0 161.0 %copy-start.100 = (f32[512]{0:T(512)}, f32[512]{0:T(512)S(1)}, u32[]{:S(2)}) copy-start(f32[512]{0:T(512)S(1)} %fusion.216) | copy-start | bytes 6148
  303.1 165.5 %copy-start.78 = (f32[512]{0:T(512)}, f32[512]{0:T(512)S(1)}, u32[]{:S(2)}) copy-start(f32[512]{0:T(512)S(1)} %broadcast_multiply_fusion.6) | copy-start | bytes 6148
  303.4 165.3 %copy-start.94 = (f32[512]{0:T(512)}, f32[512]{0:T(512)S(1)}, u32[]{:S(2)}) copy-start(f32[512]{0:T(512)S(1)} %fusion.211) | copy-start | bytes 6148
  306.1 155.0 %copy-start.70 = (f32[512]{0:T(512)}, f32[512]{0:T(512)S(1)}, u32[]{:S(2)}) copy-start(f32[512]{0:T(512)S(1)} %broadcast_multiply_fusion.5) | copy-start | bytes 6148
  307.5 153.5 %copy-start.76 = (f32[512]{0:T(512)}, f32[512]{0:T(512)S(1)}, u32[]{:S(2)}) copy-start(f32[512]{0:T(512)S(1)} %fusion.212) | copy-start | bytes 6148
  353.8 59.9 %copy-start.13 = (bf16[2,1,512,768]{3,2,1,0:T(8,128)(2,1)S(1)}, bf16[2,1,512,768]{3,2,1,0:T(8,128)(2,1)}, u32[]{:S(2)}) copy-start(bf16[2,1,512,768]{3,2,1,0:T(8,128)(2,1)} %param.33) | copy-start | bytes 4718596
  353.8 59.9 %copy-start.60 = (f32[3072]{0:T(1024)S(1)}, f32[3072]{0:T(1024)}, u32[]{:S(2)}) copy-start(f32[3072]{0:T(1024)} %convert_element_type.523) | copy-start | bytes 36868
  387.2 49.3 %copy-start.117 = (f32[512]{0:T(512)}, f32[512]{0:T(512)S(1)}, u32[]{:S(2)}) copy-start(f32[512]{0:T(512)S(1)} %broadcast_multiply_fusion.1) | copy-start | bytes 6148
  387.2 49.3 %copy-start.74 = (f32[512]{0:T(512)}, f32[512]{0:T(512)S(1)}, u32[]{:S(2)}) copy-start(f32[512]{0:T(512)S(1)} %broadcast_multiply_fusion) | copy-start | bytes 6148
  537.5 722.0 %reduce-scatter.9.cloned.1.call-start = ((), (), s32[]{:S(2)}) async-start(), calls=%async_computation.13 | async-start | bytes 14155776 | tf_op jit(solution)/shard_map/reduce_scatter | solution.py:375
  639.9 724.5 %reduce-scatter.13.cloned.1.call-start = ((), (), s32[]{:S(2)}) async-start(), calls=%async_computation.15 | async-start | bytes 2433024 | tf_op jit(solution)/shard_map/reduce_scatter | solution.py:419
  645.9 860.4 %reduce-scatter.15.cloned.1.call-start = ((), (), s32[]{:S(2)}) async-start(), calls=%async_computation.16 | async-start | bytes 9732096 | tf_op jit(solution)/shard_map/reduce_scatter | solution.py:422
  656.5 990.9 %reduce-scatter.17.cloned.1.call-start = ((), (), s32[]{:S(2)}) async-start(), calls=%async_computation.17 | async-start | bytes 9732096 | tf_op jit(solution)/shard_map/reduce_scatter | solution.py:425
  672.4 1100.3 %reduce-scatter.11.cloned.1.call-start = ((), (), s32[]{:S(2)}) async-start(), calls=%async_computation.14 | async-start | bytes 7299072 | tf_op jit(solution)/shard_map/reduce_scatter | solution.py:416
  675.3 292.0 %copy-start.5 = (bf16[2,1,512,768]{3,2,1,0:T(8,128)(2,1)S(1)}, bf16[2,1,512,768]{3,2,1,0:T(8,128)(2,1)}, u32[]{:S(2)}) copy-start(bf16[2,1,512,768]{3,2,1,0:T(8,128)(2,1)} %param.32) | copy-start | bytes 4718596
  675.3 292.0 %copy-start.73 = (f32[768]{0:T(1024)S(1)}, f32[768]{0:T(1024)}, u32[]{:S(2)}) copy-start(f32[768]{0:T(1024)} %copy-done.72) | copy-start | bytes 9220
  675.3 292.0 %copy-start.93 = (f32[512]{0:T(512)S(1)}, f32[512]{0:T(512)}, u32[]{:S(2)}) copy-start(f32[512]{0:T(512)} %copy-done.92) | copy-start | bytes 6148
  675.3 292.0 %copy-start.103 = (f32[512]{0:T(512)S(1)}, f32[512]{0:T(512)}, u32[]{:S(2)}) copy-start(f32[512]{0:T(512)} %copy-done.102) | copy-start | bytes 6148
  967.3 292.2 %copy-start.85 = (f32[512]{0:T(512)S(1)}, f32[512]{0:T(512)}, u32[]{:S(2)}) copy-start(f32[512]{0:T(512)} %copy-done.84) | copy-start | bytes 6148
  967.3 292.2 %copy-start.99 = (f32[512]{0:T(512)S(1)}, f32[512]{0:T(512)}, u32[]{:S(2)}) copy-start(f32[512]{0:T(512)} %copy-done.98) | copy-start | bytes 6148
  (128 other events, 879.4 us)
Sparse Core Ops, SparseCore 0:
  10.9 62.8 all-gather.6
  80.7 70.9 all-gather.8
  154.1 72.1 all-gather.16
  229.1 54.0 all-gather.10
  285.9 62.5 all-gather.12
  351.3 62.4 all-gather.14
  537.6 429.6 reduce-scatter.6
  970.8 288.6 reduce-scatter.8
  1265.4 98.9 reduce-scatter.12
  1371.8 134.4 reduce-scatter.14
  1512.8 134.5 reduce-scatter.16
  1654.4 118.2 reduce-scatter.10
where the time goes:
time: 1790 us; the launch traced here: 1780 us
  waiting for transfers between devices  1160 us (65%)
  matrix products  254 us (14%)
  local copies, waits for them, and re-layouts  158 us (9%)
  blocking collectives  83.6 us (5%)
  other arithmetic  74.3 us (4%)
  loops' own time  28.1 us (2%)
  between operations  18 us (1%)
    reduce_scatter x2, waiting for transfers between devices, on_device(): lax.psum_scatter(term_store.astype(jnp.float32).astype(jnp.bfloat16), 'se...  570 us
    reduce_scatter x1, waiting for transfers between devices, on_device(): lax.psum_scatter(totals[7], ('batch', 'seq'), scatter_dimension=0, tiled=...  142 us
    reduce_scatter x1, waiting for transfers between devices, on_device(): lax.psum_scatter(totals[10], ('batch', 'seq'), scatter_dimension=0, tiled...  141 us
    reduce_scatter x1, waiting for transfers between devices, on_device(): lax.psum_scatter(totals[1], ('batch', 'seq'), scatter_dimension=0, tiled=...  125 us
    unnamed x2, blocking collectives  83.6 us
    all_gather x2, waiting for transfers between devices, on_device(): gathered = lax.all_gather(key_values, 'seq', axis=1, tiled=True)  81.5 us
    unnamed x277, local copies, waits for them, and re-layouts  61.2 us
    all_gather x1, waiting for transfers between devices, fetch_params(): lax.all_gather(up_weight, ('batch', 'seq'), axis=0, tiled=True)  41 us
  transfers between devices with their start and end apart: 12, of which 11 were waited for; matrix products, arithmetic and copies ran while one was open for 20% of the time, Pallas kernels for 0%

commit v1 on v0

v1 whole, which is shorter than its diff:
```python
import math

import jax
import jax.numpy as jnp
import numpy as np
from jax import lax
from jax.experimental import pallas as pl
from jax.experimental.pallas import tpu as pltpu
from jax.sharding import Mesh
from jax.sharding import PartitionSpec as P

HEADS = 12
HD = 64
SEG = 2048
PIC = 256
HALF = SEG // 2
TILE = 256
NT = HALF // TILE
NEG = -1e30
EXP_SCALE = math.log2(math.e) / math.sqrt(HD)
SCORE_SCALE = 1.0 / math.sqrt(HD)
ALL = ("batch", "seg", "grp", "core")
F32 = jnp.float32
BF16 = jnp.bfloat16


def dot(a, b, ca, cb):
    return lax.dot_general(a, b, (((ca,), (cb,)), ((), ())), preferred_element_type=F32)


def class_base(off, number):
    parity = off if number == 0 else 1 - off
    return parity * HALF


def masked(scores, limit_row, first_key):
    keys = 2 * lax.broadcasted_iota(jnp.int32, scores.shape, 0)
    return jnp.where(keys <= limit_row - first_key, scores, NEG)


def softmax_step(state, queries, keys, values_t, shift, limit_row=None, first_key=None):
    top, total, acc = state
    scores = dot(keys, queries, 1, 0) * EXP_SCALE
    if limit_row is not None:
        scores = masked(scores, limit_row, first_key)
    new_top = jnp.maximum(top, jnp.max(scores, axis=0, keepdims=True))
    factor = jnp.exp2(top - new_top)
    weights = jnp.exp2(scores - (new_top - shift))
    total = total * factor + jnp.sum(weights, axis=0, keepdims=True)
    acc = acc * factor + dot(values_t, weights.astype(BF16), 1, 0)
    return (new_top, total, acc)


def near_forward_kernel(off_ref, flag_ref, lim_ref, q_ref, k_ref, v_ref, acc_ref, stat_ref, key_ref):
    pair = pl.program_id(0)
    for h in range(2):
        for c in range(SEG // 512):
            cols = pl.ds(c * 512, 512)
            key_ref[h, cols, :] = k_ref[h * HD : (h + 1) * HD, cols].T

    def per_tile(t, carry):
        cls = t // NT
        i = t % NT
        first = jnp.where(cls == 0, 1.0, 0.0).astype(F32)
        heads = []
        for h in range(2):
            off = off_ref[pair * 2 + h]
            own = jnp.where(cls == 0, off, 1 - off)
            base = pl.multiple_of(own * HALF + i * TILE, TILE)
            queries = q_ref[h * HD : (h + 1) * HD, pl.ds(base, TILE)]
            heads.append((off, base, queries, lim_ref[:, pl.ds(base, TILE)]))

        def step(states, other, j, use_mask):
            out = []
            for h in range(2):
                off, base, queries, limit_row = heads[h]
                parity = off if other == 0 else 1 - off
                start = pl.multiple_of(parity * HALF + j * TILE, TILE)
                keys = key_ref[h, pl.ds(start, TILE), :]
                values_t = v_ref[h * HD : (h + 1) * HD, pl.ds(start, TILE)]
                shift = first if other == 0 else 0.0
                if use_mask:
                    out.append(
                        softmax_step(
                            states[h], queries, keys, values_t, shift, limit_row, 2 * TILE * j + parity
                        )
                    )
                else:
                    out.append(softmax_step(states[h], queries, keys, values_t, shift))
            return tuple(out)

        initial = (
            jnp.full((1, TILE), NEG, F32),
            jnp.zeros((1, TILE), F32),
            jnp.zeros((HD, TILE), F32),
        )
        states = (initial, initial)
        extra = jnp.logical_and(i % 2 == 0, flag_ref[i // 2] > 0)
        for other in range(2):
            states = lax.fori_loop(0, i, lambda j, s, o=other: step(s, o, j, False), states)
            states = step(states, other, i, True)
            states = lax.cond(
                extra, lambda s, o=other: step(s, o, i + 1, True), lambda s: s, states
            )
        for h in range(2):
            base = heads[h][1]
            top, total, acc = states[h]
            acc_ref[h * HD : (h + 1) * HD, pl.ds(base, TILE)] = acc
            stat_ref[0, h : h + 1, pl.ds(base, TILE)] = top
            stat_ref[0, 2 + h : 3 + h, pl.ds(base, TILE)] = total
        return carry

    lax.fori_loop(0, 2 * NT, per_tile, 0)


def far_forward_kernel(
    off_ref, far_ref, q_ref, kx_ref, vx_ref, acc_in, stat_in, o_ref, lse_ref, key_ref
):
    pair = pl.program_id(0)
    for h in range(2):
        for c in range(HALF // 512):
            cols = pl.ds(c * 512, 512)
            key_ref[h, cols, :] = kx_ref[h * HD : (h + 1) * HD, cols].T

    def per_tile(i, carry):
        bases = []
        states = []
        for h in range(2):
            off = off_ref[pair * 2 + h]
            base = pl.multiple_of(off * HALF + i * TILE, TILE)
            rest = pl.multiple_of((1 - off) * HALF + i * TILE, TILE)
            bases.append((base, rest))
            cols = pl.ds(base, TILE)
            states.append(
                (
                    stat_in[0, h : h + 1, cols],
                    stat_in[0, 2 + h : 3 + h, cols],
                    acc_in[h * HD : (h + 1) * HD, cols],
                )
            )

        def step(j, now):
            out = []
            for h in range(2):
                start = pl.multiple_of(j * TILE, TILE)
                out.append(
                    softmax_step(
                        now[h],
                        q_ref[h * HD : (h + 1) * HD, pl.ds(bases[h][0], TILE)],
                        key_ref[h, pl.ds(start, TILE), :],
                        vx_ref[h * HD : (h + 1) * HD, pl.ds(start, TILE)],
                        0.0,
                    )
                )
            return tuple(out)

        states = lax.fori_loop(0, far_ref[0] * NT, step, tuple(states))
        for h in range(2):
            base, rest = bases[h]
            rows = slice(h * HD, (h + 1) * HD)
            top, total, acc = states[h]
            o_ref[rows, pl.ds(base, TILE)] = acc / total
            lse_ref[0, h : h + 1, pl.ds(base, TILE)] = top + jnp.log2(total)
            cols = pl.ds(rest, TILE)
            top = stat_in[0, h : h + 1, cols]
            total = stat_in[0, 2 + h : 3 + h, cols]
            o_ref[rows, cols] = acc_in[rows, cols] / total
            lse_ref[0, h : h + 1, cols] = top + jnp.log2(total)
        return carry

    lax.fori_loop(0, NT, per_tile, 0)


def slopes_step(queries, keys, values, grads, lse_row, dot_row, limit_row=None, first_key=None):
    scores = dot(keys, queries, 1, 0) * EXP_SCALE
    if limit_row is not None:
        scores = masked(scores, limit_row, first_key)
    probs = jnp.exp2(scores - lse_row)
    inner = dot(values, grads, 1, 0)
    slopes = (probs * (inner - dot_row)).astype(BF16)
    return probs.astype(BF16), slopes


def far_backward_kernel(
    off_ref,
    far_ref,
    q_ref,
    kx_ref,
    vx_ref,
    g_ref,
    o_ref,
    lse_ref,
    dq_ref,
    dkv_ref,
    key_ref,
    val_ref,
):
    pair = pl.program_id(0)

    @pl.when(far_ref[0] == 0)
    def _():
        dq_ref[...] = jnp.zeros_like(dq_ref)
        dkv_ref[...] = jnp.zeros_like(dkv_ref)

    @pl.when(far_ref[0] > 0)
    def _():
        for h in range(2):
            rows = slice(h * HD, (h + 1) * HD)
            for c in range(HALF // 512):
                cols = pl.ds(c * 512, 512)
                key_ref[h, cols, :] = kx_ref[rows, cols].T
                val_ref[h, cols, :] = vx_ref[rows, cols].T
        dq_ref[...] = jnp.zeros_like(dq_ref)

        def per_tile(j, carry):
            start = pl.multiple_of(j * TILE, TILE)
            kcols = pl.ds(start, TILE)

            def step(i, sums):
                out = []
                for h in range(2):
                    rows = slice(h * HD, (h + 1) * HD)
                    off = off_ref[pair * 2 + h]
                    qcols = pl.ds(pl.multiple_of(off * HALF + i * TILE, TILE), TILE)
                    queries = q_ref[rows, qcols]
                    grads = g_ref[rows, qcols]
                    dot_row = jnp.sum(grads.astype(F32) * o_ref[rows, qcols], axis=0, keepdims=True)
                    probs, slopes = slopes_step(
                        queries,
                        key_ref[h, kcols, :],
                        val_ref[h, kcols, :],
                        grads,
                        lse_ref[0, h : h + 1, qcols],
                        dot_row,
                    )
                    dk, dv = sums[h]
                    dk = dk + dot(queries, slopes, 1, 1)
                    dv = dv + dot(grads, probs, 1, 1)
                    out.append((dk, dv))
                    here = pl.ds(pl.multiple_of(i * TILE, TILE), TILE)
                    dq_ref[rows, here] += dot(kx_ref[rows, kcols], slopes, 1, 0)
                return tuple(out)

            zero = jnp.zeros((HD, TILE), F32)
            sums = lax.fori_loop(0, NT, step, ((zero, zero), (zero, zero)))
            for h in range(2):
                rows = slice(h * HD, (h + 1) * HD)
                dkv_ref[0, rows, kcols] = (sums[h][0] * SCORE_SCALE).astype(BF16)
                dkv_ref[1, rows, kcols] = sums[h][1].astype(BF16)
            return carry

        lax.fori_loop(0, NT, per_tile, 0)


def near_backward_kernel(
    off_ref,
    flag_ref,
    lim_ref,
    q_ref,
    k_ref,
    v_ref,
    g_ref,
    o_ref,
    lse_ref,
    dqx_ref,
    out_ref,
    key_ref,
    val_ref,
    dq_ref,
    row_ref,
):
    pair = pl.program_id(0)
    for h in range(2):
        rows = slice(h * HD, (h + 1) * HD)
        off = off_ref[pair * 2 + h]
        for c in range(SEG // 512):
            cols = pl.ds(c * 512, 512)
            key_ref[h, cols, :] = k_ref[rows, cols].T
            val_ref[h, cols, :] = v_ref[rows, cols].T
            row_ref[h : h + 1, cols] = jnp.sum(
                g_ref[rows, cols].astype(F32) * o_ref[rows, cols], axis=0, keepdims=True
            )
        active = pl.ds(pl.multiple_of(off * HALF, HALF), HALF)
        rest = pl.ds(pl.multiple_of((1 - off) * HALF, HALF), HALF)
        dq_ref[rows, active] = dqx_ref[rows, :]
        dq_ref[rows, rest] = jnp.zeros((HD, HALF), F32)

    def per_tile(t, carry):
        cls = t // NT
        j = t % NT
        first = jnp.where(cls == 0, 1.0, 0.0).astype(F32)
        starts = []
        for h in range(2):
            off = off_ref[pair * 2 + h]
            parity = jnp.where(cls == 0, off, 1 - off)
            starts.append((parity, pl.multiple_of(parity * HALF + j * TILE, TILE)))

        def step(sums, other, i, use_mask):
            out = []
            for h in range(2):
                rows = slice(h * HD, (h + 1) * HD)
                off = off_ref[pair * 2 + h]
                own = off if other == 0 else 1 - off
                qcols = pl.ds(pl.multiple_of(own * HALF + i * TILE, TILE), TILE)
                parity, start = starts[h]
                kcols = pl.ds(start, TILE)
                queries = q_ref[rows, qcols]
                grads = g_ref[rows, qcols]
                lse_row = lse_ref[0, h : h + 1, qcols]
                if other == 0:
                    lse_row = lse_row - first
                extra = (lim_ref[:, qcols], 2 * TILE * j + parity) if use_mask else ()
                probs, slopes = slopes_step(
                    queries,
                    key_ref[h, kcols, :],
                    val_ref[h, kcols, :],
                    grads,
                    lse_row,
                    row_ref[h : h + 1, qcols],
                    *extra,
                )
                dk, dv = sums[h]
                dk = dk + dot(queries, slopes, 1, 1)
                dv = dv + dot(grads, probs, 1, 1)
                out.append((dk, dv))
                dq_ref[rows, qcols] += dot(k_ref[rows, kcols], slopes, 1, 0)
            return tuple(out)

        zero = jnp.zeros((HD, TILE), F32)
        sums = ((zero, zero), (zero, zero))
        extra = jnp.logical_and(j % 2 == 1, flag_ref[j // 2] > 0)
        for other in range(2):
            sums = step(sums, other, j, True)
            sums = lax.cond(extra, lambda s, o=other: step(s, o, j - 1, True), lambda s: s, sums)
            sums = lax.fori_loop(j + 1, NT, lambda i, s, o=other: step(s, o, i, False), sums)
        for h in range(2):
            rows = slice(h * HD, (h + 1) * HD)
            kcols = pl.ds(starts[h][1], TILE)
            out_ref[1, rows, kcols] = (sums[h][0] * SCORE_SCALE).astype(BF16)
            out_ref[2, rows, kcols] = sums[h][1].astype(BF16)
        return carry

    lax.fori_loop(0, 2 * NT, per_tile, 0)
    out_ref[0] = (dq_ref[...] * SCORE_SCALE).astype(BF16)


def smem():
    return pl.BlockSpec(memory_space=pltpu.SMEM)


def rows_spec(first, width=SEG):
    return pl.BlockSpec((2 * HD, width), lambda p, f=first: (f + p, 0))


def stat_spec():
    return pl.BlockSpec((1, 8, SEG), lambda p: (p, 0, 0))


def near_forward(offsets, flags, limits, proj_t):
    pairs = offsets.shape[0] // 2
    return pl.pallas_call(
        near_forward_kernel,
        grid=(pairs,),
        in_specs=[
            smem(),
            smem(),
            pl.BlockSpec((1, SEG), lambda p: (0, 0)),
            rows_spec(0),
            rows_spec(pairs),
            rows_spec(2 * pairs),
        ],
        out_specs=[rows_spec(0), stat_spec()],
        out_shape=[
            jax.ShapeDtypeStruct((pairs * 2 * HD, SEG), F32),
            jax.ShapeDtypeStruct((pairs, 8, SEG), F32),
        ],
        scratch_shapes=[pltpu.VMEM((2, SEG, HD), BF16)],
        cost_estimate=pl.CostEstimate(
            flops=pairs * 4 * SEG * SEG * HD * 2, transcendentals=pairs * SEG * SEG, bytes_accessed=8 << 20
        ),
        name="near_forward",
    )(offsets, flags, limits, proj_t, proj_t, proj_t)


def far_forward(offsets, far, proj_t, pair_t, acc, stats):
    pairs = offsets.shape[0] // 2
    return pl.pallas_call(
        far_forward_kernel,
        grid=(pairs,),
        in_specs=[
            smem(),
            smem(),
            rows_spec(0),
            rows_spec(0, HALF),
            rows_spec(pairs, HALF),
            rows_spec(0),
            stat_spec(),
        ],
        out_specs=[rows_spec(0), stat_spec()],
        out_shape=[
            jax.ShapeDtypeStruct((pairs * 2 * HD, SEG), F32),
            jax.ShapeDtypeStruct((pairs, 8, SEG), F32),
        ],
        scratch_shapes=[pltpu.VMEM((2, HALF, HD), BF16)],
        cost_estimate=pl.CostEstimate(
            flops=pairs * 2 * SEG * SEG * HD, transcendentals=pairs * HALF * SEG, bytes_accessed=8 << 20
        ),
        name="far_forward",
    )(offsets, far, proj_t, pair_t, pair_t, acc, stats)


def far_backward(offsets, far, proj_t, pair_t, grads_t, out_t, lse):
    pairs = offsets.shape[0] // 2
    return pl.pallas_call(
        far_backward_kernel,
        grid=(pairs,),
        in_specs=[
            smem(),
            smem(),
            rows_spec(0),
            rows_spec(0, HALF),
            rows_spec(pairs, HALF),
            rows_spec(0),
            rows_spec(0),
            stat_spec(),
        ],
        out_specs=[
            rows_spec(0, HALF),
            pl.BlockSpec((2, 2 * HD, HALF), lambda p: (0, p, 0)),
        ],
        out_shape=[
            jax.ShapeDtypeStruct((pairs * 2 * HD, HALF), F32),
            jax.ShapeDtypeStruct((2, pairs * 2 * HD, HALF), BF16),
        ],
        scratch_shapes=[pltpu.VMEM((2, HALF, HD), BF16), pltpu.VMEM((2, HALF, HD), BF16)],
        cost_estimate=pl.CostEstimate(
            flops=pairs * 5 * SEG * SEG * HD, transcendentals=pairs * HALF * SEG, bytes_accessed=10 << 20
        ),
        name="far_backward",
    )(offsets, far, proj_t, pair_t, pair_t, grads_t, out_t, lse)


def near_backward(offsets, flags, limits, proj_t, grads_t, out_t, lse, dq_far):
    pairs = offsets.shape[0] // 2
    return pl.pallas_call(
        near_backward_kernel,
        grid=(pairs,),
        in_specs=[
            smem(),
            smem(),
            pl.BlockSpec((1, SEG), lambda p: (0, 0)),
            rows_spec(0),
            rows_spec(pairs),
            rows_spec(2 * pairs),
            rows_spec(0),
            rows_spec(0),
            stat_spec(),
            rows_spec(0, HALF),
        ],
        out_specs=pl.BlockSpec((3, 2 * HD, SEG), lambda p: (0, p, 0)),
        out_shape=jax.ShapeDtypeStruct((3, pairs * 2 * HD, SEG), BF16),
        scratch_shapes=[
            pltpu.VMEM((2, SEG, HD), BF16),
            pltpu.VMEM((2, SEG, HD), BF16),
            pltpu.VMEM((2 * HD, SEG), F32),
            pltpu.VMEM((8, SEG), F32),
        ],
        cost_estimate=pl.CostEstimate(
            flops=pairs * 10 * SEG * SEG * HD * 2, transcendentals=pairs * SEG * SEG, bytes_accessed=14 << 20
        ),
        name="near_backward",
    )(offsets, flags, limits, proj_t, proj_t, proj_t, grads_t, out_t, lse, dq_far)


def normalize(values):
    centred = values - jnp.mean(values, axis=-1, keepdims=True)
    spread = jnp.mean(centred * centred, axis=-1, keepdims=True)
    scale = lax.rsqrt(spread + 1e-05)
    return centred * scale, scale


def norm_back(unit, scale, gain, grad):
    scaled = grad * gain
    first = jnp.mean(scaled, axis=-1, keepdims=True)
    second = jnp.mean(scaled * unit, axis=-1, keepdims=True)
    values = (scaled - first - unit * second) * scale
    return values, jnp.sum(grad * unit, axis=0)


def gelu_and_slope(u):
    cdf = 0.5 * (1.0 + lax.erf(u * math.sqrt(0.5)))
    density = jnp.exp(-0.5 * u * u) * (1.0 / math.sqrt(2.0 * math.pi))
    return u * cdf, cdf + u * density


def flip(values, axis):
    return lax.ppermute(values, axis, [(0, 1), (1, 0)])


def spread_items(items):
    groups = lax.axis_size("grp")
    if groups != 2:
        return lax.all_to_all(items, "grp", 0, 0, tiled=True)
    me = lax.axis_index("grp")
    mine = lax.dynamic_index_in_dim(items, me, 0, keepdims=False)
    other = flip(lax.dynamic_index_in_dim(items, 1 - me, 0, keepdims=False), "grp")
    swap = me == 1
    return jnp.stack([jnp.where(swap, other, mine), jnp.where(swap, mine, other)])


def on_device(
    inputs,
    cotangent,
    pre_gain,
    qkv_weight,
    qv_bias,
    mid_gain,
    out_weight,
    out_bias,
    ffn_gain,
    up_weight,
    up_bias,
    sub_gain,
    down_weight,
    down_bias,
    pic_starts,
    head_offsets,
):
    micro, sequences, local, width = inputs.shape
    groups = lax.axis_size("grp")
    items = micro * sequences
    half = local // 2
    own_rows = groups * local
    core_heads = HEADS // 2
    core_width = core_heads * HD
    seg = lax.axis_index("seg")
    grp = lax.axis_index("grp")
    core = lax.axis_index("core")

    order = np.concatenate([np.arange(0, local, 2), np.arange(1, local, 2)])
    split = np.zeros((local, local), np.float32)
    split[np.arange(local), order] = 1.0
    split = jnp.asarray(split, BF16)

    def arrange(tokens):
        tokens = tokens.reshape(items, local, width)
        tokens = jnp.einsum("rs,isd->ird", split, tokens, preferred_element_type=F32).astype(BF16)
        tokens = spread_items(tokens)
        return tokens.reshape(groups, 2, half, width).transpose(1, 0, 2, 3)

    def restore(tokens):
        tokens = tokens.reshape(2, groups, half, width).transpose(1, 0, 2, 3)
        tokens = spread_items(tokens.reshape(groups, local, width))
        tokens = jnp.einsum("rs,ird->isd", split, tokens, preferred_element_type=F32).astype(BF16)
        return tokens.reshape(inputs.shape)

    def join_cores(own, theirs, axis):
        swap = core == 1
        return jnp.stack([jnp.where(swap, theirs, own), jnp.where(swap, own, theirs)], axis=axis)

    def gather(shard):
        return lax.all_gather(shard, ALL, axis=0, tiled=True)

    small = jnp.concatenate(
        [pre_gain, qv_bias, mid_gain, out_bias, ffn_gain, up_bias, sub_gain, down_bias]
    )
    small_all = lax.all_gather(small, ALL, axis=0).astype(F32)
    sizes = [v.shape[0] for v in (pre_gain, qv_bias, mid_gain, out_bias, ffn_gain, up_bias, sub_gain, down_bias)]
    parts = []
    at = 0
    for size in sizes:
        parts.append(small_all[:, at : at + size].reshape(-1))
        at += size
    gain_pre, bias_qv, gain_mid, bias_out, gain_ffn, bias_up, gain_sub, bias_down = parts

    weight_qkv = gather(qkv_weight).reshape(width, 3, 2, core_width)
    weight_core = lax.dynamic_index_in_dim(weight_qkv, core, 2, keepdims=False)
    weight_core = weight_core.reshape(width, 3 * core_width)
    weight_out = gather(out_weight)
    weight_up = gather(up_weight)
    weight_down = gather(down_weight)

    tokens_own = arrange(inputs)
    upstream = arrange(cotangent).reshape(own_rows, width)
    tokens_theirs = flip(tokens_own, "core")
    tokens_all = join_cores(tokens_own, tokens_theirs, 2).reshape(SEG, width).astype(F32)
    tokens_own = tokens_own.reshape(own_rows, width).astype(F32)

    unit_all, _ = normalize(tokens_all)
    normed = (unit_all * gain_pre).astype(BF16)
    bias_parts = bias_qv.reshape(2, 2, core_width)
    bias_core = lax.dynamic_index_in_dim(bias_parts, core, 1, keepdims=False)
    bias_core = jnp.concatenate([bias_core[0], jnp.zeros((core_width,), F32), bias_core[1]])
    proj_t = (
        jnp.einsum("rd,df->fr", normed, weight_core, preferred_element_type=F32)
        + bias_core[:, None]
    ).astype(BF16)

    offsets = lax.dynamic_index_in_dim(
        head_offsets.reshape(2, core_heads), core, 0, keepdims=False
    )
    starts = lax.dynamic_index_in_dim(
        pic_starts.reshape(items, pic_starts.shape[2]), grp, 0, keepdims=False
    )
    starts = starts - seg * SEG
    lane = jnp.arange(SEG, dtype=jnp.int32)
    place = 2 * (lane % HALF) + lane // HALF
    inside = (place[:, None] >= starts[None, :]) & (place[:, None] < starts[None, :] + PIC)
    ends = jnp.max(jnp.where(inside, starts[None, :] + PIC - 1, -1), axis=1)
    limits = jnp.maximum(place, ends)[None, :]
    marks = 4 * TILE * jnp.arange(NT // 2, dtype=jnp.int32) + 2 * TILE
    flags = jnp.any(
        (starts[None, :] < marks[:, None]) & (starts[None, :] + PIC > marks[:, None]), axis=1
    ).astype(jnp.int32)
    far = seg.astype(jnp.int32).reshape(1)

    pair_heads = proj_t[core_width:].reshape(2, core_heads, HD, 2, HALF)
    active = (offsets == 1)[None, :, None, None]
    pair_active = jnp.where(active, pair_heads[:, :, :, 1], pair_heads[:, :, :, 0])
    pair_active = pair_active.reshape(2 * core_width, HALF)
    pair_far = lax.ppermute(pair_active, "seg", [(0, 1)])

    acc, stats = near_forward(offsets, flags, limits, proj_t)
    out_t, lse = far_forward(offsets, far, proj_t, pair_far, acc, stats)

    def split_cores(rows):
        rows = rows.reshape(2, groups, 2, half, rows.shape[-1])
        mine = lax.dynamic_index_in_dim(rows, core, 2, keepdims=False)
        other = lax.dynamic_index_in_dim(rows, 1 - core, 2, keepdims=False)
        return mine.reshape(own_rows, -1), other.reshape(own_rows, -1)

    out_mine, out_other = split_cores(out_t.T)
    out_theirs = flip(out_other, "core")
    attended = join_cores(out_mine, out_theirs, 1).reshape(own_rows, width)

    unit_mid, scale_mid = normalize(attended)
    mid_low = (unit_mid * gain_mid).astype(BF16)
    middle = tokens_own + jnp.dot(mid_low, weight_out, preferred_element_type=F32) + bias_out
    unit_ffn, scale_ffn = normalize(middle)
    ffn_low = (unit_ffn * gain_ffn).astype(BF16)
    before = jnp.dot(ffn_low, weight_up, preferred_element_type=F32) + bias_up
    activated, slope = gelu_and_slope(before)
    unit_sub, scale_sub = normalize(activated)
    sub_low = (unit_sub * gain_sub).astype(BF16)
    finished = middle + jnp.dot(sub_low, weight_down, preferred_element_type=F32) + bias_down
    layer_out = restore(finished.astype(BF16))

    def wgrad(a, b):
        return lax.dot_general(a, b, (((0,), (0,)), ((), ())), preferred_element_type=F32)

    def back(a, w):
        return lax.dot_general(a, w, (((1,), (1,)), ((), ())), preferred_element_type=F32)

    grad_downw = wgrad(sub_low, upstream)
    grad_downb = jnp.sum(upstream.astype(F32), axis=0)
    act_grad, grad_subgain = norm_back(unit_sub, scale_sub, gain_sub, back(upstream, weight_down))
    before_grad = (act_grad * slope).astype(BF16)
    grad_upw = wgrad(ffn_low, before_grad)
    grad_upb = jnp.sum(before_grad.astype(F32), axis=0)
    middle_part, grad_ffngain = norm_back(unit_ffn, scale_ffn, gain_ffn, back(before_grad, weight_up))
    middle_grad = upstream.astype(F32) + middle_part
    branch_grad = middle_grad.astype(BF16)
    grad_outw = wgrad(mid_low, branch_grad)
    grad_outb = jnp.sum(branch_grad.astype(F32), axis=0)
    attn_grad, grad_midgain = norm_back(unit_mid, scale_mid, gain_mid, back(branch_grad, weight_out))

    attn_low = attn_grad.astype(BF16).reshape(own_rows, 2, core_width)
    keep = lax.dynamic_index_in_dim(attn_low, core, 1, keepdims=False)
    give = lax.dynamic_index_in_dim(attn_low, 1 - core, 1, keepdims=False)
    take = flip(give, "core")
    shape = (2, groups, half, core_width)
    grads_all = join_cores(keep.reshape(shape), take.reshape(shape), 2)
    grads_t = grads_all.reshape(SEG, core_width).T

    dq_far, pair_back = far_backward(offsets, far, proj_t, pair_far, grads_t, out_t, lse)
    pair_recv = lax.ppermute(pair_back, "seg", [(1, 0)])
    near = near_backward(offsets, flags, limits, proj_t, grads_t, out_t, lse, dq_far)
    near_pairs = near[1:].reshape(2, core_heads, HD, 2, HALF)
    recv = pair_recv.reshape(2, core_heads, HD, 1, HALF).astype(F32)
    chosen = offsets[None, :, None, None, None] == jnp.arange(2)[None, None, None, :, None]
    pairs_t = (near_pairs.astype(F32) + jnp.where(chosen, recv, 0.0)).astype(BF16)
    proj_grad = jnp.concatenate([near[:1], pairs_t.reshape(2, core_width, SEG)], axis=0)
    proj_grad = proj_grad.reshape(3 * core_width, SEG)

    grad_core = jnp.einsum("rd,fr->df", normed, proj_grad, preferred_element_type=F32)
    sums_core = jnp.sum(proj_grad.astype(F32), axis=1).reshape(3, core_width)
    normed_part = jnp.einsum("fr,df->rd", proj_grad, weight_core, preferred_element_type=F32)
    part_mine, part_other = split_cores(normed_part)
    part_theirs = flip(part_other.astype(BF16), "core").astype(F32)
    normed_grad = part_mine + part_theirs
    unit_own, scale_own = normalize(tokens_own)
    input_part, grad_pregain = norm_back(unit_own, scale_own, gain_pre, normed_grad)
    input_grad = restore((middle_grad + input_part).astype(BF16))

    def scatter(value):
        return lax.psum_scatter(
            value.astype(BF16), ALL, scatter_dimension=0, tiled=True
        ).astype(F32)

    own_downw = scatter(grad_downw)
    own_upw = scatter(grad_upw)
    own_outw = scatter(grad_outw)
    both = lax.psum_scatter(
        grad_core.astype(BF16), ("batch", "seg", "grp"), scatter_dimension=0, tiled=True
    )
    rows = both.shape[0] // 2
    both = both.reshape(2, rows, 3, core_width)
    mine = lax.dynamic_index_in_dim(both, core, 0, keepdims=False)
    theirs = flip(lax.dynamic_index_in_dim(both, 1 - core, 0, keepdims=False), "core")
    own_qkv = join_cores(mine, theirs, 2).reshape(rows, 6 * core_width).astype(F32)

    zeros = jnp.zeros((core_width,), F32)
    on_left = core == 0
    q_sum = jnp.concatenate([jnp.where(on_left, sums_core[0], zeros), jnp.where(on_left, zeros, sums_core[0])])
    v_sum = jnp.concatenate([jnp.where(on_left, sums_core[2], zeros), jnp.where(on_left, zeros, sums_core[2])])
    grad_qvb = jnp.concatenate([q_sum, v_sum])
    vectors = (
        grad_pregain,
        grad_qvb,
        grad_midgain,
        grad_outb,
        grad_ffngain,
        grad_upb,
        grad_subgain,
        grad_downb,
    )
    devices = small_all.shape[0]
    packed = jnp.concatenate([v.reshape(devices, -1) for v in vectors], axis=1)
    packed = lax.psum_scatter(packed, ALL, scatter_dimension=0, tiled=True)[0]
    owned = []
    at = 0
    for size in sizes:
        owned.append(packed[at : at + size])
        at += size
    return (
        layer_out,
        input_grad,
        owned[0],
        own_qkv,
        owned[1],
        owned[2],
        own_outw,
        owned[3],
        owned[4],
        own_upw,
        owned[5],
        owned[6],
        own_downw,
        owned[7],
    )


def solution(mesh):
    batch = mesh.shape["batch"]
    seq = mesh.shape["seq"]
    fine = Mesh(mesh.devices.reshape(batch, 2, seq // 4, 2), ALL)
    tokens = P(None, "batch", ("seg", "grp", "core"), None)
    vector = P(ALL)
    matrix = P(ALL, None)
    return jax.shard_map(
        on_device,
        mesh=fine,
        in_specs=(
            tokens,
            tokens,
            vector,
            matrix,
            vector,
            vector,
            matrix,
            vector,
            vector,
            matrix,
            vector,
            vector,
            matrix,
            vector,
            P(None, "batch", None),
            P(),
        ),
        out_specs=(
            tokens,
            tokens,
            vector,
            matrix,
            vector,
            vector,
            matrix,
            vector,
            vector,
            matrix,
            vector,
            vector,
            matrix,
            vector,
        ),
        check_vma=False,
    )
```

time: 1790 us -> 941 us (0.53)
  waiting for transfers between devices: 1160 us -> 234 us
  Pallas kernels: 0 us -> 183 us
  matrix products: 254 us -> 100 us
  blocking collectives: 83.6 us -> 165 us
  starting transfers between devices: 1.18 us -> 43.4 us
  local copies, waits for them, and re-layouts: 158 us -> 125 us
  loops' own time: 28.1 us -> 0 us
    reduce_scatter x6 -> x4, waiting for transfers between devices: 1000 us -> 196 us  [the longest x3 196 us: scatter(): lax.psum_scatter(value.astype(BF16), ALL, scatter_dimension=0, tiled=True)]
    pallas_call x0 -> x4, Pallas kernels: none -> 183 us  [the longest x1 86.4 us: near_backward(): pl.pallas_call(near_backward_kernel, grid=(pairs,), in_specs=[smem(), sme...]
    all_gather x6 -> x4, waiting for transfers between devices: 161 us -> 0.05 us  [gather(): return lax.all_gather(shard, ALL, axis=0, tiled=True)]
    dot_general x45 -> x16, matrix products: 254 us -> 100 us  [the longest x3 25.9 us: back(): lax.dot_general(a, w, (((1,), (1,)), ((), ())), preferred_element_type=F32)]
    unnamed x2, blocking collectives: 83.6 us -> 165 us
    ppermute x0 -> x11, starting transfers between devices: none -> 42.8 us  [the longest x9 37 us: flip(): return lax.ppermute(values, axis, [(0, 1), (1, 0)])]
    ppermute x0 -> x11, waiting for transfers between devices: none -> 35.7 us  [the longest x9 35.7 us: flip(): return lax.ppermute(values, axis, [(0, 1), (1, 0)])]
    unnamed x277 -> x131, local copies, waits for them, and re-layouts: 61.2 us -> 26.4 us
  transfers between devices with their start and end apart: 12 -> 19, of which waited for: 11 -> 4; matrix products, arithmetic and copies ran while one was open for 20% -> 23% of each run, Pallas kernels for 0% -> 19%
where the time goes in v1:
time: 941 us; the launch traced here: 931 us
  waiting for transfers between devices  234 us (25%)
  Pallas kernels  183 us (19%)
  blocking collectives  165 us (18%)
  local copies, waits for them, and re-layouts  125 us (13%)
  matrix products  100 us (11%)
  other arithmetic  65.1 us (7%)
  starting transfers between devices  43.4 us (5%)
  between operations  15.9 us (2%)
    reduce_scatter x3, waiting for transfers between devices, scatter(): lax.psum_scatter(value.astype(BF16), ALL, scatter_dimension=0, tiled=True)  196 us
    unnamed x2, blocking collectives  165 us
    pallas_call x1, Pallas kernels, near_backward(): pl.pallas_call(near_backward_kernel, grid=(pairs,), in_specs=[smem(), sme...  86.4 us
    pallas_call x1, Pallas kernels, near_forward(): pl.pallas_call(near_forward_kernel, grid=(pairs,), in_specs=[smem(), smem...  84.9 us
    ppermute x9, starting transfers between devices, flip(): return lax.ppermute(values, axis, [(0, 1), (1, 0)])  37 us
    ppermute x9, waiting for transfers between devices, flip(): return lax.ppermute(values, axis, [(0, 1), (1, 0)])  35.7 us
    unnamed x131, local copies, waits for them, and re-layouts  26.4 us
    dot_general x3, matrix products, back(): lax.dot_general(a, w, (((1,), (1,)), ((), ())), preferred_element_type=F32)  25.9 us
  transfers between devices with their start and end apart: 19, of which 4 were waited for; matrix products, arithmetic and copies ran while one was open for 23% of the time, Pallas kernels for 19%

profile of v1, /device:TPU:0, one launch (start us, length us, event | category | flops | bytes accessed | tf_op | source)
XLA Modules:
  0.0 931.1 jit_solution(14792486862423743839)
XLA Ops:
  15.2 18.2 %collective-permute-done = bf16[512,768]{0,1:T(8,128)(2,1)} collective-permute-done((bf16[512,768]{0,1:T(8,128)(2,1)S(1)}, bf16[512,768]{0,1:T(8,128)(2,1)}, u32[]{:S(2)}, u32[]{:S(2)}) %collective-permute-start) | collective-permute-done | bytes 786464 | tf_op jit(solution)/shard_map/ppermute | solution.py:497
  37.7 41.5 %all-reduce = bf16[11520]{0:T(1024)(128)(2,1)S(1)} all-reduce(bf16[11520]{0:T(1024)(128)(2,1)S(1)} %dynamic-update-slice), channel_id=2, replica_groups=mesh['batch'=4,'seg'=2,'grp'=2,'core'=2] {'batch','seg','grp','core'}, use_global_device_ids=true, to_apply=%add | all-reduce | flops 11520 | bytes 46080
  87.7 4.5 copy.132
  103.0 4.8 reshape.671
  107.8 4.5 fusion.81
  114.1 4.6 collective-permute-start.2
  120.1 84.9 %near_forward.1 = (f32[384,2048]{1,0:T(8,128)}, f32[3,8,2048]{2,1,0:T(8,128)}) custom-call(s32[6]{0:T(128)} %get-tuple-element.127.off_ref, s32[2]{0:T(128)} %convert_element_type.175.flag_ref, s32[1,2048]{1,0:T(1,128)} %fusion.57.lim_ref, bf16[1152,2048]{1,0:T(8,128)(2,1)} %copy-done.28, bf16[1152,2048]{1,0:T(8,128)(2,1)} %copy-done.28, ...), custom_call_target="tpu_custom_call" | custom-call | flops 6442450944 | bytes 8388608 | tf_op jit(solution)/shard_map/near_forward/pallas_call | solution.py:361
  206.2 5.7 far_forward.1
  216.1 11.6 %dynamic-slice_reduce_fusion.1 = (f32[2,2,256,384]{2,1,0,3:T(2,128)}, f32[2,2,256,384]{2,1,0,3:T(2,128)}) fusion(f32[2,2,2,256,384]{3,2,1,0,4:T(2,128)S(1)} %reshape.672, s32[]{:T(128)S(6)} %select_n.243, s32[]{:T(128)S(6)} %select_n.233), kind=kLoop, calls=%fused_computation.87 | loop fusion | bytes 6291464 | tf_op jit(solution)/shard_map/jit(dynamic_index_in_dim)/dynamic_slice | solution.py:629
  227.7 11.7 %reshape.673 = f32[1024,384]{0,1:T(8,128)} reshape(f32[2,2,256,384]{2,1,0,3:T(2,128)} %get-tuple-element.110) | data formatting | bytes 3145728 | tf_op jit(solution)/shard_map/reshape | solution.py:630
  240.8 16.3 %collective-permute-start.5 = (bf16[512,768]{0,1:T(8,128)(2,1)S(1)}, bf16[512,768]{0,1:T(8,128)(2,1)}, u32[]{:S(2)}, u32[]{:S(2)}) collective-permute-start(bf16[512,768]{0,1:T(8,128)(2,1)S(1)} %bitcast.277), channel_id=1, source_target_pairs={{0,2},{2,0},{1,3},{3,1},{4,6},{6,4},{5,7},{7,5},{8,10},{10,8},{9,1... | collective-permute-start | bytes 2359304 | tf_op jit(solution)/shard_map/ppermute | solution.py:497
  257.9 17.5 %collective-permute-done.5 = bf16[512,768]{0,1:T(8,128)(2,1)} collective-permute-done((bf16[512,768]{0,1:T(8,128)(2,1)S(1)}, bf16[512,768]{0,1:T(8,128)(2,1)}, u32[]{:S(2)}, u32[]{:S(2)}) %collective-permute-start.5) | collective-permute-done | bytes 786464 | tf_op jit(solution)/shard_map/ppermute | solution.py:497
  291.4 12.1 %fusion.78 = (f32[1024]{0:T(1024)S(1)}, f32[1024,3072]{1,0:T(8,128)S(1)}, f32[1024,3072]{1,0:T(8,128)}) fusion(f32[3072]{0:T(1024)S(1)} %add.258, bf16[768,3072]{1,0:T(8,128)(2,1)} %all-gather.10.cloned.1.call-done, f32[1024,768]{1,0:T(8,128)} %copy-done.13, f32[768]{0:T(1024)S(1)} %mul.318, f32[1024]{0:T(1024)S(1)} %add_rsqrt_fusion.2, ...), kind=kOutput, calls=%fused_computation.213 | convolution fusion | flops 4853857280 | bytes 33057792 | tf_op jit(solution)/shard_map/dot_general | solution.py:641
  303.4 4.5 copy-done.2
  309.3 13.7 %multiply_reduce_fusion = (f32[3072]{0:T(1024)S(1)}, f32[1024]{0:T(1024)S(1)}, f32[1024]{0:T(1024)S(1)}, f32[1024,3072]{1,0:T(8,128)}) fusion(f32[1024,3072]{1,0:T(8,128)} %copy-done.2, f32[1024]{0:T(1024)S(1)} %add_rsqrt_fusion.1, f32[1024]{0:T(1024)S(1)} %broadcast_multiply_fusion.4, f32[3072]{0:T(1024)S(1)} %mul.329, bf16[1024,768]{1,0:T(8,128)(2,1)} %bitcast.258, ...), kind=kOutput, calls=%fused_computation.7 | convolution fusion | flops 4856998912 | bytes 31498240 | tf_op jit(solution)/shard_map/dot_general | solution.py:652
  323.0 18.9 %convert_reduce_fusion = (f32[3072]{0:T(1024)S(1)}, bf16[1024,3072]{1,0:T(8,128)(2,1)S(1)}, bf16[1024,3072]{1,0:T(8,128)(2,1)}) fusion(f32[1024,3072]{1,0:T(8,128)} %get-tuple-element.179, f32[3072]{0:T(1024)S(1)} %add.258, f32[1024]{0:T(1024)S(1)} %broadcast_multiply_fusion.2, f32[1024]{0:T(1024)S(1)} %add_rsqrt_fusion.1, f32[1024,3072]{1,0:T(8,128)} %copy-done.2, ...), kind=kLoop, calls=%fused_computation.8 | loop fusion | flops 69202944 | bytes 50384896 | tf_op jit(solution)/shard_map/reduce_sum | solution.py:659
  341.9 10.2 %multiply_reduce_fusion.4 = (f32[768]{0:T(1024)S(1)}, f32[1024]{0:T(1024)S(1)}, f32[1024]{0:T(1024)S(1)}, f32[1024,768]{1,0:T(8,128)S(1)}) fusion(f32[1024,768]{1,0:T(8,128)S(1)} %copy-done.14, f32[1024]{0:T(1024)S(1)} %add_rsqrt_fusion.2, f32[1024]{0:T(1024)S(1)} %broadcast_multiply_fusion.11, f32[768]{0:T(1024)S(1)} %mul.318, ...), kind=kOutput, calls=%fused_computation.53 | convolution fusion | flops 4838126592 | bytes 17324032 | tf_op jit(solution)/shard_map/dot_general | solution.py:652
  364.9 5.7 far_backward.1
  375.7 86.4 %near_backward.1 = bf16[3,384,2048]{2,1,0:T(8,128)(2,1)} custom-call(s32[6]{0:T(128)} %get-tuple-element.127.off_ref, s32[2]{0:T(128)} %convert_element_type.175.flag_ref, s32[1,2048]{1,0:T(1,128)} %fusion.57.lim_ref, bf16[1152,2048]{1,0:T(8,128)(2,1)} %copy-done.28, bf16[1152,2048]{1,0:T(8,128)(2,1)} %copy-done.28, bf16[1152,2048]{1,0:T(8,128)(2,1)} %copy-done.28, ...), custom_call_target="tpu_custom_call" | custom-call | flops 16106127360 | bytes 14680064 | tf_op jit(solution)/shard_map/near_backward/pallas_call | solution.py:445
  463.7 6.3 broadcast_in_dim.58
  470.1 9.3 broadcast_in_dim.59
  479.4 5.1 add_convert_fusion.1
  488.8 8.0 convolution_convert_fusion.2
  496.9 9.9 %convolution_convert_fusion.1 = bf16[768,3072]{1,0:T(8,128)(2,1)} fusion(bf16[1024,3072]{1,0:T(8,128)(2,1)} %copy-done.23, f32[1024,768]{1,0:T(8,128)S(1)} %copy-done.15, f32[768]{0:T(1024)S(1)} %mul.318, f32[1024]{0:T(1024)S(1)} %add_rsqrt_fusion.2, f32[1024]{0:T(1024)S(1)} %broadcast_multiply_fusion.11), kind=kOutput, calls=%fused_computation.27 | convolution fusion | flops 4837343232 | bytes 14167040 | tf_op jit(solution)/shard_map/dot_general | solution.py:649
  509.6 9.1 convolution_convert_fusion
  518.7 6.8 copy.146
  525.6 6.1 fusion.85
  535.9 8.5 add_convert_fusion.2
  559.2 17.0 %collective-permute-start.4 = (bf16[512,768]{0,1:T(8,128)(2,1)}, bf16[512,768]{0,1:T(8,128)(2,1)}, u32[]{:S(2)}, u32[]{:S(2)}) collective-permute-start(bf16[512,768]{0,1:T(8,128)(2,1)} %bitcast.276), channel_id=1, source_target_pairs={{0,2},{2,0},{1,3},{3,1},{4,6},{6,4},{5,7},{7,5},{8,10},{10,8},{9,1... | collective-permute-start | bytes 2359304 | tf_op jit(solution)/shard_map/ppermute | solution.py:497
  581.2 123.9 %all-reduce.1 = f32[32,360]{1,0:T(8,128)S(1)} all-reduce(f32[32,360]{1,0:T(8,128)S(1)} %concatenate.22), channel_id=3, replica_groups=mesh['batch'=4,'seg'=2,'grp'=2,'core'=2] {'batch','seg','grp','core'}, use_global_device_ids=true, to_apply=%region_29.30.clone | all-reduce | flops 11520 | bytes 92160
  724.9 84.7 %reduce-scatter.9.cloned.1.call-done = bf16[24,3072]{1,0:T(8,128)(2,1)} async-done(((bf16[768,3072]{1,0:T(8,128)(2,1)}), bf16[24,3072]{1,0:T(8,128)(2,1)}) %reduce-scatter.9.cloned.1.call-update) | async-done | bytes 147472 | tf_op jit(solution)/shard_map/reduce_scatter | solution.py:696
  811.3 110.8 %reduce-scatter.11.cloned.1.call-done = bf16[96,768]{1,0:T(8,128)(2,1)} async-done(((bf16[3072,768]{1,0:T(8,128)(2,1)}), bf16[96,768]{1,0:T(8,128)(2,1)}) %reduce-scatter.11.cloned.1.call-update) | async-done | bytes 147472 | tf_op jit(solution)/shard_map/reduce_scatter | solution.py:696
  (304 shorter events, 132.4 us)
Async XLA Ops:
  7.2 80.5 %all-gather.6.cloned.1.call-start = ((), (), s32[]{:S(2)}) async-start(), calls=%async_computation.4 | async-start | bytes 3649536 | tf_op jit(solution)/shard_map/all_gather | solution.py:562
  7.9 277.2 %all-gather.8.cloned.1.call-start = ((), (), s32[]{:S(2)}) async-start(), calls=%async_computation.5 | async-start | bytes 1216512 | tf_op jit(solution)/shard_map/all_gather | solution.py:562
  8.7 282.7 %all-gather.10.cloned.1.call-start = ((), (), s32[]{:S(2)}) async-start(), calls=%async_computation.6 | async-start | bytes 4866048 | tf_op jit(solution)/shard_map/all_gather | solution.py:562
  9.4 299.9 %all-gather.12.cloned.1.call-start = ((), (), s32[]{:S(2)}) async-start(), calls=%async_computation.7 | async-start | bytes 4866048 | tf_op jit(solution)/shard_map/all_gather | solution.py:562
  11.9 21.4 %collective-permute-start = (bf16[512,768]{0,1:T(8,128)(2,1)S(1)}, bf16[512,768]{0,1:T(8,128)(2,1)}, u32[]{:S(2)}, u32[]{:S(2)}) collective-permute-start(bf16[512,768]{0,1:T(8,128)(2,1)S(1)} %copy.127), channel_id=1, source_target_pairs={{0,2},{2,0},{1,3},{3,1},{4,6},{6,4},{5,7},{7,5},{8,10},{10,8},{9,1... | collective-permute-start | bytes 2359304 | tf_op jit(solution)/shard_map/ppermute | solution.py:497
  34.7 46.1 %copy-start.54 = (s32[2,1,4]{2,1,0:T(1,128)S(1)}, s32[2,1,4]{2,1,0:T(1,128)}, u32[]{:S(2)}) copy-start(s32[2,1,4]{2,1,0:T(1,128)} %param.31) | copy-start | bytes 100
  35.0 48.6 %copy-start.3 = (bf16[512,768]{1,0:T(8,128)(2,1)}, bf16[512,768]{1,0:T(8,128)(2,1)S(1)}, u32[]{:S(2)}) copy-start(bf16[512,768]{1,0:T(8,128)(2,1)S(1)} %copy.158) | copy-start | bytes 2359300
  35.3 48.3 %copy-start.5 = (bf16[512,768]{1,0:T(8,128)(2,1)}, bf16[512,768]{1,0:T(8,128)(2,1)S(1)}, u32[]{:S(2)}) copy-start(bf16[512,768]{1,0:T(8,128)(2,1)S(1)} %copy.159) | copy-start | bytes 2359300
  35.5 48.1 %copy-start.31 = (bf16[2,2,256,768]{3,2,1,0:T(8,128)(2,1)}, bf16[2,2,256,768]{3,2,1,0:T(8,128)(2,1)S(1)}, u32[]{:S(2)}) copy-start(bf16[2,2,256,768]{3,2,1,0:T(8,128)(2,1)S(1)} %maximum_bitcast_fusion) | copy-start | bytes 4718596
  35.5 46.5 %collective-permute-start.1 = (bf16[2,2,256,768]{3,2,1,0:T(8,128)(2,1)S(1)}, bf16[2,2,256,768]{3,2,1,0:T(8,128)(2,1)}, u32[]{:S(2)}, u32[]{:S(2)}) collective-permute-start(bf16[2,2,256,768]{3,2,1,0:T(8,128)(2,1)S(1)} %maximum_bitcast_fusion), channel_id=1, source_target_pairs={{0,1},{1,0},{2,3},{3,2},{4,5},{5,4},{6,7},{7,6},{8,9},{9,8},{10,11... | collective-permute-start | bytes 4718600 | tf_op jit(solution)/shard_map/ppermute | solution.py:497
  35.6 510.5 %reduce-scatter.7.cloned.1.call-start = ((), (), s32[]{:S(2)}) async-start(), calls=%async_computation.9 | async-start | bytes 1216512 | tf_op jit(solution)/shard_map/reduce_scatter | solution.py:696
  114.1 90.9 %collective-permute-start.2 = (bf16[768,1024]{1,0:T(8,128)(2,1)S(1)}, bf16[768,1024]{1,0:T(8,128)(2,1)S(1)}, u32[]{:S(2)}, u32[]{:S(2)}) collective-permute-start(bf16[768,1024]{1,0:T(8,128)(2,1)S(1)} %bitcast_select_fusion), channel_id=1, source_target_pairs={{0,4},{1,5},{2,6},{3,7},{8,12},{9,13},{10,14},{11,15},{16,20},{17,... | collective-permute-start | bytes 4718600 | tf_op jit(solution)/shard_map/ppermute | solution.py:621
  227.7 11.7 %copy-start.58 = (bf16[512,512,1]{1,0,2:T(8,128)(2,1)S(1)}, bf16[512,512,1]{1,0,2:T(8,128)(2,1)}, u32[]{:S(2)}) copy-start(bf16[512,512,1]{1,0,2:T(8,128)(2,1)} %constant.190) | copy-start | bytes 1572868
  239.4 41.8 %collective-permute-start.3 = (f32[1024,384]{0,1:T(8,128)}, f32[1024,384]{0,1:T(8,128)}, u32[]{:S(2)}, u32[]{:S(2)}) collective-permute-start(f32[1024,384]{0,1:T(8,128)} %reshape.673), channel_id=1, source_target_pairs={{0,1},{1,0},{2,3},{3,2},{4,5},{5,4},{6,7},{7,6},{8,9},{9,8},{10,11... | collective-permute-start | bytes 4718600 | tf_op jit(solution)/shard_map/ppermute | solution.py:497
  240.4 16.7 %copy-start.34 = (f32[32,360]{1,0:T(8,128)S(1)}, f32[32,360]{1,0:T(8,128)}, u32[]{:S(2)}) copy-start(f32[32,360]{1,0:T(8,128)} %copy-done.33) | copy-start | bytes 138244
  240.4 16.9 %copy-start.39 = (f32[32,24]{1,0:T(8,128)S(1)}, f32[32,24]{1,0:T(8,128)}, u32[]{:S(2)}) copy-start(f32[32,24]{1,0:T(8,128)} %get-tuple-element.169) | copy-start | bytes 9220
  240.4 17.0 %copy-start.38 = (f32[32,24]{1,0:T(8,128)S(1)}, f32[32,24]{1,0:T(8,128)}, u32[]{:S(2)}) copy-start(f32[32,24]{1,0:T(8,128)} %get-tuple-element.171) | copy-start | bytes 9220
  240.8 34.6 %collective-permute-start.5 = (bf16[512,768]{0,1:T(8,128)(2,1)S(1)}, bf16[512,768]{0,1:T(8,128)(2,1)}, u32[]{:S(2)}, u32[]{:S(2)}) collective-permute-start(bf16[512,768]{0,1:T(8,128)(2,1)S(1)} %bitcast.277), channel_id=1, source_target_pairs={{0,2},{2,0},{1,3},{3,1},{4,6},{6,4},{5,7},{7,5},{8,10},{10,8},{9,1... | collective-permute-start | bytes 2359304 | tf_op jit(solution)/shard_map/ppermute | solution.py:497
  323.0 18.9 %copy-start.14 = (f32[1024,768]{1,0:T(8,128)S(1)}, f32[1024,768]{1,0:T(8,128)}, u32[]{:S(2)}) copy-start(f32[1024,768]{1,0:T(8,128)} %copy-done.13) | copy-start | bytes 9437188
  357.5 2.9 collective-permute-start.6
  370.6 93.2 %collective-permute-start.7 = (bf16[2,384,1024]{2,1,0:T(8,128)(2,1)}, bf16[2,384,1024]{2,1,0:T(8,128)(2,1)}, u32[]{:S(2)}, u32[]{:S(2)}) collective-permute-start(bf16[2,384,1024]{2,1,0:T(8,128)(2,1)} %get-tuple-element.25), channel_id=1, source_target_pairs={{4,0},{5,1},{6,2},{7,3},{12,8},{13,9},{14,10},{15,11},{20,16},{21,... | collective-permute-start | bytes 4718600 | tf_op jit(solution)/shard_map/ppermute | solution.py:676
  375.7 339.5 %reduce-scatter.5.cloned.1.call-start = ((), (), s32[]{:S(2)}) async-start(), calls=%async_computation.8 | async-start | bytes 1880064 | tf_op jit(solution)/shard_map/reduce_scatter | solution.py:703
  463.7 20.8 %copy-start.12 = (bf16[1,384,2048]{2,1,0:T(8,128)(2,1)}, bf16[1,384,2048]{2,1,0:T(8,128)(2,1)S(1)}, u32[]{:S(2)}) copy-start(bf16[1,384,2048]{2,1,0:T(8,128)(2,1)S(1)} %slice.157) | copy-start | bytes 4718596
  496.8 312.9 %reduce-scatter.9.cloned.1.call-start = ((), (), s32[]{:S(2)}) async-start(), calls=%async_computation.10 | async-start | bytes 4866048 | tf_op jit(solution)/shard_map/reduce_scatter | solution.py:696
  506.8 415.3 %reduce-scatter.11.cloned.1.call-start = ((), (), s32[]{:S(2)}) async-start(), calls=%async_computation.11 | async-start | bytes 4866048 | tf_op jit(solution)/shard_map/reduce_scatter | solution.py:696
  531.7 12.8 %copy-start.24 = (f32[2,2,2,256,768]{4,3,2,1,0:T(8,128)}, f32[2,2,2,256,768]{4,3,2,1,0:T(8,128)S(1)}, u32[]{:S(2)}) copy-start(f32[2,2,2,256,768]{4,3,2,1,0:T(8,128)S(1)} %fusion.85) | copy-start | bytes 18874372
  533.0 16.6 %collective-permute-start.8 = (bf16[1024,768]{1,0:T(8,128)(2,1)}, bf16[1024,768]{1,0:T(8,128)(2,1)S(1)}, u32[]{:S(2)}, u32[]{:S(2)}) collective-permute-start(bf16[1024,768]{1,0:T(8,128)(2,1)} %bitcast.53), channel_id=1, source_target_pairs={{0,1},{1,0},{2,3},{3,2},{4,5},{5,4},{6,7},{7,6},{8,9},{9,8},{10,11... | collective-permute-start | bytes 4718600 | tf_op jit(solution)/shard_map/ppermute | solution.py:497
  554.8 21.4 %copy-start.11 = (bf16[2,384,2048]{2,1,0:T(8,128)(2,1)S(1)}, bf16[2,384,2048]{2,1,0:T(8,128)(2,1)}, u32[]{:S(2)}) copy-start(bf16[2,384,2048]{2,1,0:T(8,128)(2,1)} %copy-done.10) | copy-start | bytes 9437188
  559.2 150.5 %collective-permute-start.4 = (bf16[512,768]{0,1:T(8,128)(2,1)}, bf16[512,768]{0,1:T(8,128)(2,1)}, u32[]{:S(2)}, u32[]{:S(2)}) collective-permute-start(bf16[512,768]{0,1:T(8,128)(2,1)} %bitcast.276), channel_id=1, source_target_pairs={{0,2},{2,0},{1,3},{3,1},{4,6},{6,4},{5,7},{7,5},{8,10},{10,8},{9,1... | collective-permute-start | bytes 2359304 | tf_op jit(solution)/shard_map/ppermute | solution.py:497
  581.1 132.0 %collective-permute-start.9 = (bf16[512,768]{0,1:T(8,128)(2,1)}, bf16[512,768]{0,1:T(8,128)(2,1)}, u32[]{:S(2)}, u32[]{:S(2)}) collective-permute-start(bf16[512,768]{0,1:T(8,128)(2,1)} %bitcast.57), channel_id=1, source_target_pairs={{0,2},{2,0},{1,3},{3,1},{4,6},{6,4},{5,7},{7,5},{8,10},{10,8},{9,1... | collective-permute-start | bytes 2359304 | tf_op jit(solution)/shard_map/ppermute | solution.py:497
  716.2 7.7 collective-permute-start.10
  719.7 204.1 %copy-start.1 = (bf16[2,1,512,768]{3,2,1,0:T(8,128)(2,1)S(1)}, bf16[2,1,512,768]{3,2,1,0:T(8,128)(2,1)}, u32[]{:S(2)}) copy-start(bf16[2,1,512,768]{3,2,1,0:T(8,128)(2,1)} %param.17) | copy-start | bytes 4718596
  (46 other events, 173.1 us)
Sparse Core Ops, SparseCore 0:
  10.9 63.0 all-gather.5
  76.9 52.9 all-gather.7
  132.8 64.7 all-gather.9
  200.4 65.1 all-gather.11
  375.8 154.9 reduce-scatter.6
  535.5 162.7 reduce-scatter.4
  703.7 105.9 reduce-scatter.8
  816.1 106.0 reduce-scatter.10

commit v2 on v1

v2 whole, which is shorter than its diff:
```python
import math

import jax
import jax.numpy as jnp
import numpy as np
from jax import lax
from jax.experimental import pallas as pl
from jax.experimental.pallas import tpu as pltpu
from jax.sharding import Mesh
from jax.sharding import PartitionSpec as P

HEADS = 12
HD = 64
SEG = 2048
PIC = 256
HALF = SEG // 2
TILE = 512
NT = HALF // TILE
NEG = -1e30
SAFE_EXPONENT = 100.0
EXP_SCALE = math.log2(math.e) / math.sqrt(HD)
SCORE_SCALE = 1.0 / math.sqrt(HD)
ALL = ("batch", "seg", "grp", "core")
F32 = jnp.float32
BF16 = jnp.bfloat16


def dot(a, b, ca, cb):
    return lax.dot_general(a, b, (((ca,), (cb,)), ((), ())), preferred_element_type=F32)


def class_lanes(off, number, tile):
    parity = off if number == 0 else 1 - off
    return parity, pl.ds(pl.multiple_of(parity * HALF + tile * TILE, TILE), TILE)


def masked(scores, limit_row, first_key):
    keys = 2 * lax.broadcasted_iota(jnp.int32, scores.shape, 0)
    return jnp.where(keys <= limit_row - first_key, scores, NEG)


def plain_step(state, scores, values_t):
    top, total, acc = state
    weights = jnp.exp2(scores)
    total = total + jnp.sum(weights, axis=0, keepdims=True)
    acc = acc + dot(values_t, weights.astype(BF16), 1, 0)
    return (top, total, acc)


def online_step(state, scores, values_t):
    top, total, acc = state
    new_top = jnp.maximum(top, jnp.max(scores, axis=0, keepdims=True))
    factor = jnp.exp2(top - new_top)
    weights = jnp.exp2(scores - new_top)
    total = total * factor + jnp.sum(weights, axis=0, keepdims=True)
    acc = acc * factor + dot(values_t, weights.astype(BF16), 1, 0)
    return (new_top, total, acc)


def longest(values_t):
    wide = values_t.astype(F32)
    return jnp.max(jnp.sum(wide * wide, axis=0, keepdims=True))


def scores_bounded(queries_t, keys_t):
    square = longest(queries_t) * longest(keys_t) * (EXP_SCALE * EXP_SCALE)
    return square < SAFE_EXPONENT * SAFE_EXPONENT


def near_forward_kernel(off_ref, lim_ref, q_ref, k_ref, v_ref, acc_ref, stat_ref, key_ref):
    pair = pl.program_id(0)
    for h in range(2):
        for c in range(SEG // TILE):
            cols = pl.ds(c * TILE, TILE)
            key_ref[h, cols, :] = k_ref[h * HD : (h + 1) * HD, cols].T
    bounded = scores_bounded(q_ref[...], k_ref[...])

    def run(step, begin):
        def per_class(cls, carry):
            first = jnp.where(cls == 0, 1.0, 0.0).astype(F32)
            for i in range(NT):
                heads = []
                for h in range(2):
                    off = off_ref[pair * 2 + h]
                    own = jnp.where(cls == 0, off, 1 - off)
                    cols = pl.ds(pl.multiple_of(own * HALF + i * TILE, TILE), TILE)
                    heads.append((off, cols, q_ref[h * HD : (h + 1) * HD, cols], lim_ref[:, cols]))
                states = [
                    (jnp.full((1, TILE), begin, F32), jnp.zeros((1, TILE), F32), jnp.zeros((HD, TILE), F32))
                ] * 2
                for other in range(2):
                    for j in range(i + 1):
                        for h in range(2):
                            off, cols, queries, limit_row = heads[h]
                            parity, kcols = class_lanes(off, other, j)
                            scores = dot(key_ref[h, kcols, :], queries, 1, 0) * EXP_SCALE
                            if other == 0:
                                scores = scores + first
                            if j == i:
                                scores = masked(scores, limit_row, 2 * TILE * j + parity)
                            states[h] = step(states[h], scores, v_ref[h * HD : (h + 1) * HD, kcols])
                for h in range(2):
                    cols = heads[h][1]
                    top, total, acc = states[h]
                    acc_ref[h * HD : (h + 1) * HD, cols] = acc
                    stat_ref[0, h : h + 1, cols] = top
                    stat_ref[0, 2 + h : 3 + h, cols] = total
            return carry

        lax.fori_loop(0, 2, per_class, 0)

    @pl.when(bounded)
    def _():
        run(plain_step, 0.0)
        stat_ref[0, 4:5, :] = jnp.ones((1, SEG), F32)

    @pl.when(jnp.logical_not(bounded))
    def _():
        run(online_step, NEG)
        stat_ref[0, 4:5, :] = jnp.zeros((1, SEG), F32)


def far_forward_kernel(
    off_ref, far_ref, q_ref, kx_ref, vx_ref, acc_in, stat_in, ot_ref, lse_ref, o_ref, key_ref
):
    pair = pl.program_id(0)
    has_far = far_ref[0] > 0
    bounded = jnp.logical_and(
        scores_bounded(q_ref[...], kx_ref[...]), jnp.max(stat_in[0, 4:5, 0:128]) > 0.5
    )

    def finish(cols, h, state):
        rows = slice(h * HD, (h + 1) * HD)
        top, total, acc = state
        ot_ref[rows, cols] = acc / total
        lse_ref[0, h : h + 1, cols] = top + jnp.log2(total)

    def state_of(cols, h):
        return (
            stat_in[0, h : h + 1, cols],
            stat_in[0, 2 + h : 3 + h, cols],
            acc_in[h * HD : (h + 1) * HD, cols],
        )

    def run(step, width):
        for h in range(2):
            for c in range(HALF // TILE):
                cols = pl.ds(c * TILE, TILE)
                key_ref[h, cols, :] = kx_ref[h * HD : (h + 1) * HD, cols].T
        for i in range(HALF // width):
            lanes = []
            states = []
            for h in range(2):
                off = off_ref[pair * 2 + h]
                cols = pl.ds(pl.multiple_of(off * HALF + i * width, width), width)
                lanes.append(cols)
                states.append(state_of(cols, h))
            for j in range(NT):
                for h in range(2):
                    rows = slice(h * HD, (h + 1) * HD)
                    kcols = pl.ds(j * TILE, TILE)
                    scores = dot(key_ref[h, kcols, :], q_ref[rows, lanes[h]], 1, 0) * EXP_SCALE
                    states[h] = step(states[h], scores, vx_ref[rows, kcols])
            for h in range(2):
                finish(lanes[h], h, states[h])

    @pl.when(jnp.logical_and(has_far, bounded))
    def _():
        run(plain_step, HALF)

    @pl.when(jnp.logical_and(has_far, jnp.logical_not(bounded)))
    def _():
        run(online_step, TILE)

    @pl.when(jnp.logical_not(has_far))
    def _():
        for h in range(2):
            cols = pl.ds(pl.multiple_of(off_ref[pair * 2 + h] * HALF, HALF), HALF)
            finish(cols, h, state_of(cols, h))

    for h in range(2):
        cols = pl.ds(pl.multiple_of((1 - off_ref[pair * 2 + h]) * HALF, HALF), HALF)
        finish(cols, h, state_of(cols, h))
    for c in range(SEG // TILE):
        cols = pl.ds(c * TILE, TILE)
        o_ref[cols, :] = ot_ref[:, cols].T


def slopes_of(scores, lse_row, inner, dot_row):
    probs = jnp.exp2(scores - lse_row)
    return probs.astype(BF16), (probs * (inner - dot_row)).astype(BF16)


def far_backward_kernel(
    off_ref,
    far_ref,
    q_ref,
    kx_ref,
    vx_ref,
    g_ref,
    ot_ref,
    lse_ref,
    dq_ref,
    dkv_ref,
    key_ref,
    val_ref,
    gt_ref,
    acc_ref,
):
    pair = pl.program_id(0)

    @pl.when(far_ref[0] == 0)
    def _():
        dq_ref[...] = jnp.zeros_like(dq_ref)
        dkv_ref[...] = jnp.zeros_like(dkv_ref)

    @pl.when(far_ref[0] > 0)
    def _():
        for c in range(SEG // TILE):
            gt_ref[:, pl.ds(c * TILE, TILE)] = g_ref[pl.ds(c * TILE, TILE), :].T
        for h in range(2):
            rows = slice(h * HD, (h + 1) * HD)
            for c in range(HALF // TILE):
                cols = pl.ds(c * TILE, TILE)
                key_ref[h, cols, :] = kx_ref[rows, cols].T
                val_ref[h, cols, :] = vx_ref[rows, cols].T
        for h in range(2):
            rows = slice(h * HD, (h + 1) * HD)
            off = off_ref[pair * 2 + h]
            qcols = pl.ds(pl.multiple_of(off * HALF, HALF), HALF)
            queries = q_ref[rows, qcols]
            grads = gt_ref[rows, qcols]
            lse_row = lse_ref[0, h : h + 1, qcols]
            dot_row = jnp.sum(grads.astype(F32) * ot_ref[rows, qcols], axis=0, keepdims=True)
            total = jnp.zeros((HD, HALF), F32)
            for j in range(NT):
                kcols = pl.ds(j * TILE, TILE)
                scores = dot(key_ref[h, kcols, :], queries, 1, 0) * EXP_SCALE
                inner = dot(val_ref[h, kcols, :], grads, 1, 0)
                probs, slopes = slopes_of(scores, lse_row, inner, dot_row)
                acc_ref[rows, kcols] = (dot(queries, slopes, 1, 1) * SCORE_SCALE).astype(BF16)
                acc_ref[2 * HD + h * HD : 2 * HD + (h + 1) * HD, kcols] = dot(grads, probs, 1, 1).astype(BF16)
                total = total + dot(kx_ref[rows, kcols], slopes, 1, 0)
            dq_ref[rows, :] = total
        for c in range(HALF // TILE):
            cols = pl.ds(c * TILE, TILE)
            dkv_ref[0, cols, :] = acc_ref[: 2 * HD, cols].T
            dkv_ref[1, cols, :] = acc_ref[2 * HD :, cols].T


def near_backward_kernel(
    off_ref,
    lim_ref,
    q_ref,
    k_ref,
    v_ref,
    g_ref,
    ot_ref,
    lse_ref,
    dqx_ref,
    out_q_ref,
    out_ref,
    key_ref,
    val_ref,
    gt_ref,
    dq_ref,
    row_ref,
    acc_ref,
):
    pair = pl.program_id(0)
    for c in range(SEG // TILE):
        gt_ref[:, pl.ds(c * TILE, TILE)] = g_ref[pl.ds(c * TILE, TILE), :].T
    for h in range(2):
        rows = slice(h * HD, (h + 1) * HD)
        off = off_ref[pair * 2 + h]
        for c in range(SEG // TILE):
            cols = pl.ds(c * TILE, TILE)
            key_ref[h, cols, :] = k_ref[rows, cols].T
            val_ref[h, cols, :] = v_ref[rows, cols].T
            row_ref[h : h + 1, cols] = jnp.sum(
                gt_ref[rows, cols].astype(F32) * ot_ref[rows, cols], axis=0, keepdims=True
            )
        active = pl.ds(pl.multiple_of(off * HALF, HALF), HALF)
        rest = pl.ds(pl.multiple_of((1 - off) * HALF, HALF), HALF)
        dq_ref[rows, active] = dqx_ref[rows, :]
        dq_ref[rows, rest] = jnp.zeros((HD, HALF), F32)

    def per_class(cls, carry):
        first = jnp.where(cls == 0, 1.0, 0.0).astype(F32)
        for j in range(NT):
            lanes = []
            for h in range(2):
                off = off_ref[pair * 2 + h]
                parity = jnp.where(cls == 0, off, 1 - off)
                lanes.append((parity, pl.ds(pl.multiple_of(parity * HALF + j * TILE, TILE), TILE)))
            sums = [(jnp.zeros((HD, TILE), F32), jnp.zeros((HD, TILE), F32))] * 2
            for other in range(2):
                for i in range(j, NT):
                    for h in range(2):
                        rows = slice(h * HD, (h + 1) * HD)
                        parity, kcols = lanes[h]
                        _, qcols = class_lanes(off_ref[pair * 2 + h], other, i)
                        queries = q_ref[rows, qcols]
                        grads = gt_ref[rows, qcols]
                        lse_row = lse_ref[0, h : h + 1, qcols]
                        if other == 0:
                            lse_row = lse_row - first
                        scores = dot(key_ref[h, kcols, :], queries, 1, 0) * EXP_SCALE
                        if i == j:
                            scores = masked(scores, lim_ref[:, qcols], 2 * TILE * j + parity)
                        inner = dot(val_ref[h, kcols, :], grads, 1, 0)
                        probs, slopes = slopes_of(scores, lse_row, inner, row_ref[h : h + 1, qcols])
                        dk, dv = sums[h]
                        sums[h] = (dk + dot(queries, slopes, 1, 1), dv + dot(grads, probs, 1, 1))
                        dq_ref[rows, qcols] += dot(k_ref[rows, kcols], slopes, 1, 0)
            for h in range(2):
                rows = slice(h * HD, (h + 1) * HD)
                kcols = lanes[h][1]
                acc_ref[rows, kcols] = (sums[h][0] * SCORE_SCALE).astype(BF16)
                acc_ref[2 * HD + h * HD : 2 * HD + (h + 1) * HD, kcols] = sums[h][1].astype(BF16)
        return carry

    lax.fori_loop(0, 2, per_class, 0)
    for c in range(SEG // TILE):
        cols = pl.ds(c * TILE, TILE)
        out_q_ref[cols, :] = (dq_ref[:, cols] * SCORE_SCALE).astype(BF16).T
        out_ref[0, cols, :] = acc_ref[: 2 * HD, cols].T
        out_ref[1, cols, :] = acc_ref[2 * HD :, cols].T


def smem():
    return pl.BlockSpec(memory_space=pltpu.SMEM)


def rows_spec(first, width=SEG):
    return pl.BlockSpec((2 * HD, width), lambda p, f=first: (f + p, 0))


def cols_spec():
    return pl.BlockSpec((SEG, 2 * HD), lambda p: (0, p))


def stat_spec():
    return pl.BlockSpec((1, 8, SEG), lambda p: (p, 0, 0))


def limit_spec():
    return pl.BlockSpec((1, SEG), lambda p: (0, 0))


def cost(pairs, matmuls, scores, size):
    return pl.CostEstimate(
        flops=pairs * 2 * matmuls * 2 * HD * scores, transcendentals=pairs * 2 * scores, bytes_accessed=size
    )


def near_forward(offsets, limits, proj_t):
    pairs = offsets.shape[0] // 2
    return pl.pallas_call(
        near_forward_kernel,
        grid=(pairs,),
        in_specs=[smem(), limit_spec(), rows_spec(0), rows_spec(pairs), rows_spec(2 * pairs)],
        out_specs=[rows_spec(0), stat_spec()],
        out_shape=[
            jax.ShapeDtypeStruct((pairs * 2 * HD, SEG), F32),
            jax.ShapeDtypeStruct((pairs, 8, SEG), F32),
        ],
        scratch_shapes=[pltpu.VMEM((2, SEG, HD), BF16)],
        cost_estimate=cost(pairs, 8, 3 * HALF * HALF, 8 << 20),
        name="near_forward",
    )(offsets, limits, proj_t, proj_t, proj_t)


def far_forward(offsets, far, proj_t, pair_t, acc, stats):
    pairs = offsets.shape[0] // 2
    return pl.pallas_call(
        far_forward_kernel,
        grid=(pairs,),
        in_specs=[
            smem(),
            smem(),
            rows_spec(0),
            rows_spec(0, HALF),
            rows_spec(pairs, HALF),
            rows_spec(0),
            stat_spec(),
        ],
        out_specs=[rows_spec(0), stat_spec(), cols_spec()],
        out_shape=[
            jax.ShapeDtypeStruct((pairs * 2 * HD, SEG), F32),
            jax.ShapeDtypeStruct((pairs, 8, SEG), F32),
            jax.ShapeDtypeStruct((SEG, pairs * 2 * HD), F32),
        ],
        scratch_shapes=[pltpu.VMEM((2, HALF, HD), BF16)],
        cost_estimate=cost(pairs, 8, HALF * HALF, 12 << 20),
        name="far_forward",
    )(offsets, far, proj_t, pair_t, pair_t, acc, stats)


def far_backward(offsets, far, proj_t, pair_t, grads, out_t, lse):
    pairs = offsets.shape[0] // 2
    return pl.pallas_call(
        far_backward_kernel,
        grid=(pairs,),
        in_specs=[
            smem(),
            smem(),
            rows_spec(0),
            rows_spec(0, HALF),
            rows_spec(pairs, HALF),
            cols_spec(),
            rows_spec(0),
            stat_spec(),
        ],
        out_specs=[
            rows_spec(0, HALF),
            pl.BlockSpec((2, HALF, 2 * HD), lambda p: (0, 0, p)),
        ],
        out_shape=[
            jax.ShapeDtypeStruct((pairs * 2 * HD, HALF), F32),
            jax.ShapeDtypeStruct((2, HALF, pairs * 2 * HD), BF16),
        ],
        scratch_shapes=[
            pltpu.VMEM((2, HALF, HD), BF16),
            pltpu.VMEM((2, HALF, HD), BF16),
            pltpu.VMEM((2 * HD, SEG), BF16),
            pltpu.VMEM((4 * HD, HALF), BF16),
        ],
        cost_estimate=cost(pairs, 20, HALF * HALF, 10 << 20),
        name="far_backward",
    )(offsets, far, proj_t, pair_t, pair_t, grads, out_t, lse)


def near_backward(offsets, limits, proj_t, grads, out_t, lse, dq_far):
    pairs = offsets.shape[0] // 2
    return pl.pallas_call(
        near_backward_kernel,
        grid=(pairs,),
        in_specs=[
            smem(),
            limit_spec(),
            rows_spec(0),
            rows_spec(pairs),
            rows_spec(2 * pairs),
            cols_spec(),
            rows_spec(0),
            stat_spec(),
            rows_spec(0, HALF),
        ],
        out_specs=[cols_spec(), pl.BlockSpec((2, SEG, 2 * HD), lambda p: (0, 0, p))],
        out_shape=[
            jax.ShapeDtypeStruct((SEG, pairs * 2 * HD), BF16),
            jax.ShapeDtypeStruct((2, SEG, pairs * 2 * HD), BF16),
        ],
        scratch_shapes=[
            pltpu.VMEM((2, SEG, HD), BF16),
            pltpu.VMEM((2, SEG, HD), BF16),
            pltpu.VMEM((2 * HD, SEG), BF16),
            pltpu.VMEM((2 * HD, SEG), F32),
            pltpu.VMEM((8, SEG), F32),
            pltpu.VMEM((4 * HD, SEG), BF16),
        ],
        cost_estimate=cost(pairs, 20, 3 * HALF * HALF, 14 << 20),
        name="near_backward",
    )(offsets, limits, proj_t, proj_t, proj_t, grads, out_t, lse, dq_far)


def normalize(values):
    centred = values - jnp.mean(values, axis=-1, keepdims=True)
    spread = jnp.mean(centred * centred, axis=-1, keepdims=True)
    scale = lax.rsqrt(spread + 1e-05)
    return centred * scale, scale


def norm_back(unit, scale, gain, grad):
    scaled = grad * gain
    first = jnp.mean(scaled, axis=-1, keepdims=True)
    second = jnp.mean(scaled * unit, axis=-1, keepdims=True)
    values = (scaled - first - unit * second) * scale
    return values, jnp.sum(grad * unit, axis=0)


def gelu_and_slope(u):
    cdf = 0.5 * (1.0 + lax.erf(u * math.sqrt(0.5)))
    density = jnp.exp(-0.5 * u * u) * (1.0 / math.sqrt(2.0 * math.pi))
    return u * cdf, cdf + u * density


def flip(values, axis):
    return lax.ppermute(values, axis, [(0, 1), (1, 0)])


def spread_items(items):
    groups = lax.axis_size("grp")
    if groups != 2:
        return lax.all_to_all(items, "grp", 0, 0, tiled=True)
    me = lax.axis_index("grp")
    mine = lax.dynamic_index_in_dim(items, me, 0, keepdims=False)
    other = flip(lax.dynamic_index_in_dim(items, 1 - me, 0, keepdims=False), "grp")
    swap = me == 1
    return jnp.stack([jnp.where(swap, other, mine), jnp.where(swap, mine, other)])


def shifted(values, amount):
    count = lax.axis_size("batch")
    return lax.ppermute(values, "batch", [(i, (i + amount) % count) for i in range(count)])


def across(values, ds, dg):
    table = [(2 * s + g, 2 * (s ^ ds) + (g ^ dg)) for s in range(2) for g in range(2)]
    return lax.ppermute(values, ("seg", "grp"), table)


OTHERS = ((1, 0), (0, 1), (1, 1))


def together(*values):
    return lax.optimization_barrier(values)


def column_pieces(shard):
    return [shifted(shard, k) for k in range(1, lax.axis_size("batch"))]


def column_place(own, pieces):
    count = lax.axis_size("batch")
    batch = lax.axis_index("batch")
    column = jnp.zeros((count,) + own.shape, own.dtype)
    for k, piece in enumerate([own] + list(pieces)):
        column = lax.dynamic_update_index_in_dim(column, piece, (batch + count - k) % count, 0)
    return column


def plane_pieces(values):
    return [across(values, ds, dg) for ds, dg in OTHERS]


def plane_place(own, pieces):
    seg, grp = lax.axis_index("seg"), lax.axis_index("grp")
    plane = jnp.zeros((2, 2) + own.shape, own.dtype)
    zero = jnp.zeros((), jnp.int32)
    for (ds, dg), piece in zip(((0, 0),) + OTHERS, [own] + list(pieces)):
        place = (seg ^ ds, grp ^ dg) + (zero,) * own.ndim
        plane = lax.dynamic_update_slice(plane, piece[None, None], place)
    return plane


def plane_part(parts, ds, dg):
    seg, grp = lax.axis_index("seg"), lax.axis_index("grp")
    rows = lax.dynamic_index_in_dim(parts, seg ^ ds, 0, keepdims=False)
    return lax.dynamic_index_in_dim(rows, grp ^ dg, 0, keepdims=False)


def plane_sends(parts):
    return [across(plane_part(parts, ds, dg), ds, dg) for ds, dg in OTHERS]


def plane_sum(parts, received):
    total = plane_part(parts, 0, 0).astype(F32)
    for piece in received:
        total = total + piece.astype(F32)
    return total


def column_sends(column):
    count = lax.axis_size("batch")
    batch = lax.axis_index("batch")
    low = column.astype(BF16)
    return [
        shifted(lax.dynamic_index_in_dim(low, (batch + k) % count, 0, keepdims=False), k)
        for k in range(1, count)
    ]


def column_sum(column, received):
    total = lax.dynamic_index_in_dim(column, lax.axis_index("batch"), 0, keepdims=False)
    for piece in received:
        total = total + piece.astype(F32)
    return total


def on_device(
    inputs,
    cotangent,
    pre_gain,
    qkv_weight,
    qv_bias,
    mid_gain,
    out_weight,
    out_bias,
    ffn_gain,
    up_weight,
    up_bias,
    sub_gain,
    down_weight,
    down_bias,
    pic_starts,
    head_offsets,
):
    micro, sequences, local, width = inputs.shape
    groups = lax.axis_size("grp")
    items = micro * sequences
    half = local // 2
    own_rows = groups * local
    core_heads = HEADS // 2
    core_width = core_heads * HD
    batches = lax.axis_size("batch")
    seg = lax.axis_index("seg")
    grp = lax.axis_index("grp")
    core = lax.axis_index("core")
    staged = groups == 2

    order = np.concatenate([np.arange(0, local, 2), np.arange(1, local, 2)])
    split = np.zeros((local, local), np.float32)
    split[np.arange(local), order] = 1.0
    split = jnp.asarray(split, BF16)

    def arrange(tokens):
        tokens = spread_items(tokens.reshape(items, local, width))
        tokens = jnp.einsum("rs,isd->ird", split, tokens, preferred_element_type=F32).astype(BF16)
        return tokens.reshape(groups, 2, half, width).transpose(1, 0, 2, 3)

    def restore(tokens):
        tokens = tokens.reshape(2, groups, half, width).transpose(1, 0, 2, 3)
        tokens = spread_items(tokens.reshape(groups, local, width))
        tokens = jnp.einsum("rs,ird->isd", split, tokens, preferred_element_type=F32).astype(BF16)
        return tokens.reshape(inputs.shape)

    def join_cores(own, theirs, axis):
        swap = core == 1
        return jnp.stack([jnp.where(swap, theirs, own), jnp.where(swap, own, theirs)], axis=axis)

    rows = qkv_weight.shape[0]
    ff = up_weight.shape[1]
    cut = width // 2

    def column_halves(value):
        size = value.shape[1] // 2
        return [lax.dynamic_slice_in_dim(value, i * size, size, 1) for i in (core, 1 - core)]

    def core_rows(values):
        halves = [column_halves(value) for value in values]
        mine, other = (jnp.concatenate([half[i] for half in halves], axis=1) for i in range(2))
        both = join_cores(mine, flip(other, "core"), 0)
        return both.reshape(-1, both.shape[2])

    def whole_columns(own, other):
        swap = core == 1
        return jnp.concatenate([jnp.where(swap, other, own), jnp.where(swap, own, other)], axis=1)

    def library_gather(shard):
        whole = lax.all_gather(shard, ("batch", "seg", "grp"), axis=0)
        return whole.reshape(-1, shard.shape[1])

    tokens_own = spread_items(inputs.reshape(items, local, width))

    vectors = (pre_gain, qv_bias, mid_gain, out_bias, ffn_gain, up_bias, sub_gain, down_bias)
    counts = [v.shape[0] // rows for v in vectors]
    small = jnp.concatenate([v.reshape(rows, -1) for v in vectors], axis=1)
    small = jnp.pad(small, ((0, 0), (0, 128 - small.shape[1])))
    halves = qkv_weight.reshape(rows, 3, 2, core_width)
    mine = lax.dynamic_index_in_dim(halves, core, 2, keepdims=False)
    other = lax.dynamic_index_in_dim(halves, 1 - core, 2, keepdims=False)
    mine = jnp.concatenate([mine.reshape(rows, -1), small], axis=1)
    other = jnp.concatenate([other.reshape(rows, -1), small], axis=1)
    first = join_cores(mine, flip(other, "core"), 0).reshape(2 * rows, -1)
    wide = core_rows([out_weight, up_weight])
    deep = core_rows([down_weight])

    if staged:
        column = column_place(first, column_pieces(first))
        wide_plane = plane_place(wide, plane_pieces(wide))
        wide_plane, deep_shard, column = together(wide_plane, deep, column)
        wide_pieces = column_pieces(wide_plane)
        deep_pieces = column_pieces(deep_shard)
        first = plane_place(column, plane_pieces(column))
        first = first.transpose(2, 0, 1, 3, 4).reshape(width, -1)
    else:
        first = library_gather(first)

    tokens_own = jnp.einsum("rs,isd->ird", split, tokens_own, preferred_element_type=F32).astype(BF16)
    tokens_own = tokens_own.reshape(groups, 2, half, width).transpose(1, 0, 2, 3)
    tokens_theirs = flip(tokens_own, "core")
    tokens_all = join_cores(tokens_own, tokens_theirs, 2).reshape(SEG, width).astype(F32)
    tokens_own = tokens_own.reshape(own_rows, width).astype(F32)
    unit_all, _ = normalize(tokens_all)

    if staged:
        first, unit_all, wide_pieces[0], wide_pieces[-1] = together(
            first, unit_all, wide_pieces[0], wide_pieces[-1]
        )
    weight_core = first[:, : 3 * core_width]
    small_all = first[:, 3 * core_width :].astype(F32)
    parts = []
    at = 0
    for count in counts:
        parts.append(small_all[:, at : at + count].reshape(-1))
        at += count
    gain_pre, bias_qv, gain_mid, bias_out, gain_ffn, bias_up, gain_sub, bias_down = parts
    normed = (unit_all * gain_pre).astype(BF16)
    bias_parts = bias_qv.reshape(2, 2, core_width)
    bias_core = lax.dynamic_index_in_dim(bias_parts, core, 1, keepdims=False)
    bias_core = jnp.concatenate([bias_core[0], jnp.zeros((core_width,), F32), bias_core[1]])
    proj_t = (
        jnp.einsum("rd,df->fr", normed, weight_core, preferred_element_type=F32)
        + bias_core[:, None]
    ).astype(BF16)

    offsets = lax.dynamic_index_in_dim(
        head_offsets.reshape(2, core_heads), core, 0, keepdims=False
    )
    starts = lax.dynamic_index_in_dim(
        pic_starts.reshape(items, pic_starts.shape[2]), grp, 0, keepdims=False
    )
    starts = starts - seg * SEG
    lane = jnp.arange(SEG, dtype=jnp.int32)
    place = 2 * (lane % HALF) + lane // HALF
    inside = (place[:, None] >= starts[None, :]) & (place[:, None] < starts[None, :] + PIC)
    ends = jnp.max(jnp.where(inside, starts[None, :] + PIC - 1, -1), axis=1)
    limits = jnp.maximum(place, ends)[None, :]
    far = seg.astype(jnp.int32).reshape(1)

    odd_rows = jnp.tile(jnp.repeat(offsets, HD), 2) == 1
    pairs_all = proj_t[core_width:]
    pair_active = jnp.where(odd_rows[:, None], pairs_all[:, HALF:], pairs_all[:, :HALF])
    pair_far = lax.ppermute(pair_active, "seg", [(0, 1)])

    acc, stats = near_forward(offsets, limits, proj_t)
    if staged:
        cotangent, acc, stats, pair_far, deep_pieces, wide_pieces = together(
            cotangent, acc, stats, pair_far, deep_pieces, wide_pieces
        )
        wide_own = column_place(wide_plane, wide_pieces).reshape(width, -1)
        deep_column = column_place(deep, deep_pieces)
        deep_planes = plane_pieces(deep_column)
    else:
        wide_own = library_gather(wide)
        deep_own = library_gather(deep)
    wide_other = flip(wide_own, "core")
    upstream = arrange(cotangent).reshape(own_rows, width)
    out_t, lse, out_rows = far_forward(offsets, far, proj_t, pair_far, acc, stats)

    def split_cores(rows):
        rows = rows.reshape(2, groups, 2, half, rows.shape[-1])
        mine = lax.dynamic_index_in_dim(rows, core, 2, keepdims=False)
        other = lax.dynamic_index_in_dim(rows, 1 - core, 2, keepdims=False)
        return mine.reshape(own_rows, -1), other.reshape(own_rows, -1)

    out_mine, out_other = split_cores(out_rows)
    out_theirs = flip(out_other, "core")
    attended = join_cores(out_mine, out_theirs, 1).reshape(own_rows, width)
    weight_out = whole_columns(wide_own[:, :cut], wide_other[:, :cut])
    weight_up = whole_columns(wide_own[:, cut:], wide_other[:, cut:])

    unit_mid, scale_mid = normalize(attended)
    mid_low = (unit_mid * gain_mid).astype(BF16)
    middle = tokens_own + jnp.dot(mid_low, weight_out, preferred_element_type=F32) + bias_out
    unit_ffn, scale_ffn = normalize(middle)
    ffn_low = (unit_ffn * gain_ffn).astype(BF16)
    before = jnp.dot(ffn_low, weight_up, preferred_element_type=F32) + bias_up
    if staged:
        before, upstream, deep_planes = together(before, upstream, deep_planes)
        deep_own = plane_place(deep_column, deep_planes)
        deep_own = deep_own.transpose(2, 0, 1, 3, 4).reshape(ff, -1)
    deep_other = flip(deep_own, "core")
    weight_down = whole_columns(deep_own, deep_other)
    activated, slope = gelu_and_slope(before)
    unit_sub, scale_sub = normalize(activated)
    sub_low = (unit_sub * gain_sub).astype(BF16)
    finished = middle + jnp.dot(sub_low, weight_down, preferred_element_type=F32) + bias_down
    layer_out = restore(finished.astype(BF16))

    def wgrad(a, b):
        return lax.dot_general(a, b, (((0,), (0,)), ((), ())), preferred_element_type=F32)

    def back(a, w):
        return lax.dot_general(a, w, (((1,), (1,)), ((), ())), preferred_element_type=F32)

    grad_downw = wgrad(sub_low, upstream)
    grad_downb = jnp.sum(upstream.astype(F32), axis=0)
    act_grad, grad_subgain = norm_back(unit_sub, scale_sub, gain_sub, back(upstream, weight_down))
    before_grad = (act_grad * slope).astype(BF16)
    grad_upw = wgrad(ffn_low, before_grad)
    grad_upb = jnp.sum(before_grad.astype(F32), axis=0)
    middle_part, grad_ffngain = norm_back(unit_ffn, scale_ffn, gain_ffn, back(before_grad, weight_up))
    middle_grad = upstream.astype(F32) + middle_part
    branch_grad = middle_grad.astype(BF16)
    grad_outw = wgrad(mid_low, branch_grad)
    grad_outb = jnp.sum(branch_grad.astype(F32), axis=0)
    attn_grad, grad_midgain = norm_back(unit_mid, scale_mid, gain_mid, back(branch_grad, weight_out))

    def core_sum(values):
        halves = [column_halves(value.astype(BF16)) for value in values]
        mine, other = (jnp.concatenate([half[i] for half in halves], axis=1) for i in range(2))
        summed = (mine.astype(F32) + flip(other, "core").astype(F32)).astype(BF16)
        per_chip = summed.shape[0] // (batches * 2 * groups)
        return summed.reshape(batches, 2, groups, per_chip, -1).transpose(1, 2, 0, 3, 4)

    def library_scatter(parts):
        flat = parts.transpose(2, 0, 1, 3, 4).reshape((-1,) + parts.shape[3:])
        return lax.psum_scatter(flat, ("batch", "seg", "grp"), scatter_dimension=0).astype(F32)

    attn_low = attn_grad.astype(BF16).reshape(own_rows, 2, core_width)
    keep = lax.dynamic_index_in_dim(attn_low, core, 1, keepdims=False)
    give = lax.dynamic_index_in_dim(attn_low, 1 - core, 1, keepdims=False)
    take = flip(give, "core")
    deep_parts = core_sum([grad_downw])
    wide_parts = core_sum([grad_outw, grad_upw])
    if staged:
        take, deep_parts, wide_parts = together(take, deep_parts, wide_parts)
        deep_received = plane_sends(deep_parts)
        wide_received = plane_sends(wide_parts)
    shape = (2, groups, half, core_width)
    grads_all = join_cores(keep.reshape(shape), take.reshape(shape), 2)
    grads_rows = grads_all.reshape(SEG, core_width)

    dq_far, pair_back = far_backward(offsets, far, proj_t, pair_far, grads_rows, out_t, lse)
    pair_recv = lax.ppermute(pair_back, "seg", [(1, 0)])
    if staged:
        dq_far, deep_received = together(dq_far, deep_received)
        deep_column = plane_sum(deep_parts, deep_received)
        deep_sends = column_sends(deep_column)
    grad_q, grad_near = near_backward(offsets, limits, proj_t, grads_rows, out_t, lse, dq_far)
    if staged:
        grad_q, grad_near, pair_recv, deep_sends, wide_received = together(
            grad_q, grad_near, pair_recv, deep_sends, wide_received
        )
        deep_total = column_sum(deep_column, deep_sends)
        wide_column = plane_sum(wide_parts, wide_received)
        wide_total = column_sum(wide_column, column_sends(wide_column))
    else:
        deep_total = library_scatter(deep_parts)
        wide_total = library_scatter(wide_parts)
    parity = lax.broadcasted_iota(jnp.int32, (1, 2, 1, 1), 1)
    chosen = jnp.repeat(offsets, HD)[None, None, None, :] == parity
    grad_pair = grad_near.reshape(2, 2, HALF, core_width).astype(F32)
    grad_pair = grad_pair + jnp.where(chosen, pair_recv[:, None].astype(F32), 0.0)
    grad_pair = grad_pair.astype(BF16).reshape(2, SEG, core_width)
    proj_grads = (grad_q, grad_pair[0], grad_pair[1])
    weight_cols = [weight_core[:, i * core_width : (i + 1) * core_width] for i in range(3)]
    grad_core = jnp.concatenate([wgrad(normed, g).astype(BF16) for g in proj_grads], axis=1)
    sums_core = [jnp.sum(g.astype(F32), axis=0) for g in proj_grads]
    normed_part = back(proj_grads[0], weight_cols[0])
    normed_part = normed_part + back(proj_grads[1], weight_cols[1]) + back(proj_grads[2], weight_cols[2])
    part_mine, part_other = split_cores(normed_part)
    part_theirs = flip(part_other.astype(BF16), "core").astype(F32)
    normed_grad = part_mine + part_theirs
    unit_own, scale_own = normalize(tokens_own)
    input_part, grad_pregain = norm_back(unit_own, scale_own, gain_pre, normed_grad)
    input_grad = restore((middle_grad + input_part).astype(BF16))

    def finish_halves(total, cuts):
        total = total.reshape(2, total.shape[0] // 2, -1)
        mine = lax.dynamic_index_in_dim(total, core, 0, keepdims=False)
        theirs = lax.dynamic_index_in_dim(total, 1 - core, 0, keepdims=False)
        theirs = flip(theirs.astype(BF16), "core").astype(F32)
        out = []
        at = 0
        for cut in cuts:
            out.append(whole_columns(mine[:, at : at + cut], theirs[:, at : at + cut]))
            at += cut
        return out

    own_outw, own_upw = finish_halves(wide_total, [cut, ff // 2])
    own_downw = finish_halves(deep_total, [cut])[0]

    zeros = jnp.zeros((core_width,), F32)
    on_left = core == 0
    q_sum = jnp.concatenate([jnp.where(on_left, sums_core[0], zeros), jnp.where(on_left, zeros, sums_core[0])])
    v_sum = jnp.concatenate([jnp.where(on_left, sums_core[2], zeros), jnp.where(on_left, zeros, sums_core[2])])
    grad_qvb = jnp.concatenate([q_sum, v_sum])
    vector_grads = (
        grad_pregain,
        grad_qvb,
        grad_midgain,
        grad_outb,
        grad_ffngain,
        grad_upb,
        grad_subgain,
        grad_downb,
    )
    packed = jnp.concatenate([v.reshape(width, -1) for v in vector_grads], axis=1)
    packed = jnp.pad(packed, ((0, 0), (0, 128 - packed.shape[1])))
    tail = jnp.concatenate([grad_core, packed.astype(BF16)], axis=1)
    tail = tail.reshape(batches, 2, groups, 2 * rows, -1).transpose(1, 2, 0, 3, 4)
    if staged:
        tail_column = plane_sum(tail, plane_sends(tail))
        tail = column_sum(tail_column, column_sends(tail_column))
    else:
        tail = library_scatter(tail)
    tail = tail.reshape(2, rows, -1)
    mine = lax.dynamic_index_in_dim(tail, core, 0, keepdims=False)
    theirs = lax.dynamic_index_in_dim(tail, 1 - core, 0, keepdims=False)
    theirs = flip(theirs.astype(BF16), "core").astype(F32)
    columns = 3 * core_width
    own_qkv = join_cores(
        mine[:, :columns].reshape(rows, 3, core_width), theirs[:, :columns].reshape(rows, 3, core_width), 2
    ).reshape(rows, 2 * columns)
    own_small = mine[:, columns:] + theirs[:, columns:]
    owned = []
    at = 0
    for count in counts:
        owned.append(own_small[:, at : at + count].reshape(-1))
        at += count
    return (
        layer_out,
        input_grad,
        owned[0],
        own_qkv,
        owned[1],
        owned[2],
        own_outw,
        owned[3],
        owned[4],
        own_upw,
        owned[5],
        owned[6],
        own_downw,
        owned[7],
    )


def solution(mesh):
    batch = mesh.shape["batch"]
    seq = mesh.shape["seq"]
    fine = Mesh(mesh.devices.reshape(batch, 2, seq // 4, 2), ALL)
    tokens = P(None, "batch", ("seg", "grp", "core"), None)
    vector = P(ALL)
    matrix = P(ALL, None)
    return jax.shard_map(
        on_device,
        mesh=fine,
        in_specs=(
            tokens,
            tokens,
            vector,
            matrix,
            vector,
            vector,
            matrix,
            vector,
            vector,
            matrix,
            vector,
            vector,
            matrix,
            vector,
            P(None, "batch", None),
            P(),
        ),
        out_specs=(
            tokens,
            tokens,
            vector,
            matrix,
            vector,
            vector,
            matrix,
            vector,
            vector,
            matrix,
            vector,
            vector,
            matrix,
            vector,
        ),
        check_vma=False,
    )
```

time: 941 us -> 559 us (0.59)
  blocking collectives: 165 us -> 0 us
  waiting for transfers between devices: 234 us -> 100 us
  Pallas kernels: 183 us -> 101 us
  other arithmetic: 65.1 us -> 94 us
  starting transfers between devices: 43.4 us -> 71.6 us
  local copies, waits for them, and re-layouts: 125 us -> 101 us
  matrix products: 100 us -> 82.2 us
  between operations: 15.9 us -> 2.94 us
    reduce_scatter x4 -> x0, waiting for transfers between devices: 196 us -> none  [the longest x3 196 us: scatter(): lax.psum_scatter(value.astype(BF16), ALL, scatter_dimension=0, tiled=True)]
    unnamed x2 -> x0, blocking collectives: 165 us -> none
    ppermute x0 -> x36, waiting for transfers between devices: none -> 85.2 us  [the longest x18 52.9 us: across(): return lax.ppermute(values, ('seg', 'grp'), table)]
    pallas_call x2, Pallas kernels: 171 us -> 87.9 us  [the longest x1 60.3 us: near_backward(): pl.pallas_call(near_backward_kernel, grid=(pairs,), in_specs=[smem(), lim...]
    ppermute x0 -> x36, starting transfers between devices: none -> 59.1 us  [the longest x18 29.6 us: shifted(): lax.ppermute(values, 'batch', [(i, (i + amount) % count) for i in range(c...]
    ppermute x9 -> x18, starting transfers between devices: 37 us -> 7.47 us  [flip(): return lax.ppermute(values, axis, [(0, 1), (1, 0)])]
    ppermute x9 -> x18, waiting for transfers between devices: 35.7 us -> 13.6 us  [flip(): return lax.ppermute(values, axis, [(0, 1), (1, 0)])]
    dynamic_update_slice x0 -> x24, local copies, waits for them, and re-layouts: none -> 19.5 us  [the longest x12 11.3 us: column_place(): lax.dynamic_update_index_in_dim(column, piece, (batch + count - k) % coun...]
  transfers between devices with their start and end apart: 19 -> 56, of which waited for: 4 -> 26; matrix products, arithmetic and copies ran while one was open for 23% -> 29% of each run, Pallas kernels for 19% -> 17%
where the time goes in v2:
time: 559 us; the launch traced here: 553 us
  local copies, waits for them, and re-layouts  101 us (18%)
  Pallas kernels  101 us (18%)
  waiting for transfers between devices  100 us (18%)
  other arithmetic  94 us (17%)
  matrix products  82.2 us (15%)
  starting transfers between devices  71.6 us (13%)
    pallas_call x1, Pallas kernels, near_backward(): pl.pallas_call(near_backward_kernel, grid=(pairs,), in_specs=[smem(), lim...  60.3 us
    ppermute x18, waiting for transfers between devices, across(): return lax.ppermute(values, ('seg', 'grp'), table)  52.9 us
    ppermute x18, waiting for transfers between devices, shifted(): lax.ppermute(values, 'batch', [(i, (i + amount) % count) for i in range(c...  32.3 us
    dot_general x6, matrix products, back(): lax.dot_general(a, w, (((1,), (1,)), ((), ())), preferred_element_type=F32)  31.4 us
    ppermute x18, starting transfers between devices, shifted(): lax.ppermute(values, 'batch', [(i, (i + amount) % count) for i in range(c...  29.6 us
    ppermute x18, starting transfers between devices, across(): return lax.ppermute(values, ('seg', 'grp'), table)  29.5 us
    pallas_call x1, Pallas kernels, near_forward(): pl.pallas_call(near_forward_kernel, grid=(pairs,), in_specs=[smem(), limi...  27.6 us
    dot_general x6, matrix products, wgrad(): lax.dot_general(a, b, (((0,), (0,)), ((), ())), preferred_element_type=F32)  22.4 us
  transfers between devices with their start and end apart: 56, of which 26 were waited for; matrix products, arithmetic and copies ran while one was open for 29% of the time, Pallas kernels for 17%

profile of v2, /device:TPU:0, one launch (start us, length us, event | category | flops | bytes accessed | tf_op | source)
XLA Modules:
  0.0 552.6 jit_solution(686852645118070900)
XLA Ops:
  32.7 5.6 %collective-permute-done.3 = bf16[48,1920]{1,0:T(8,128)(2,1)S(1)} collective-permute-done((bf16[48,1920]{1,0:T(8,128)(2,1)S(1)}, bf16[48,1920]{1,0:T(8,128)(2,1)S(1)}, u32[]{:S(2)}, u32[]{:S(2)}) %collective-permute-start.3) | collective-permute-done | bytes 184352 | tf_op jit(solution)/shard_map/ppermute | solution.py:511
  38.4 4.9 collective-permute-done.4
  59.6 8.3 %collective-permute-done.12 = bf16[4,48,1280]{2,1,0:T(8,128)(2,1)S(1)} collective-permute-done((bf16[4,48,1280]{2,1,0:T(8,128)(2,1)S(1)}, bf16[4,48,1280]{2,1,0:T(8,128)(2,1)S(1)}, u32[]{:S(2)}, u32[]{:S(2)}) %collective-permute-start.12) | collective-permute-done | bytes 491552 | tf_op jit(solution)/shard_map/ppermute | solution.py:511
  79.4 6.5 %collective-permute-start.20 = (bf16[2,2,48,1920]{3,2,1,0:T(8,128)(2,1)S(1)}, bf16[2,2,48,1920]{3,2,1,0:T(8,128)(2,1)}, u32[]{:S(2)}, u32[]{:S(2)}) collective-permute-start(bf16[2,2,48,1920]{3,2,1,0:T(8,128)(2,1)S(1)} %bitcast_dynamic-update-slice_fusion.12), channel_id=1, source_target_pairs={{0,16},{8,24},{16,0},{24,8},{1,17},{9,25},{17,1},{25,9},{2,18},{10... | collective-permute-start | bytes 2211848 | tf_op jit(solution)/shard_map/ppermute | solution.py:506
  91.3 4.5 add_convert_fusion.q_ref.k_ref.v_ref
  98.4 3.8 collective-permute-start.16
  102.3 27.6 %near_forward.1 = (f32[384,2048]{1,0:T(8,128)}, f32[3,8,2048]{2,1,0:T(8,128)}) custom-call(s32[6]{0:T(128)} %copy-done.76, s32[1,2048]{1,0:T(1,128)} %fusion.90.lim_ref, bf16[1152,2048]{1,0:T(8,128)(2,1)} %copy-done.27, bf16[1152,2048]{1,0:T(8,128)(2,1)} %copy-done.27, bf16[1152,2048]{1,0:T(8,128)(2,1)} %copy-done.27), custom_call_target="tpu_custom_call" | custom-call | flops 19327352832 | bytes 8388608 | tf_op jit(solution)/shard_map/near_forward/pallas_call | solution.py:359
  132.4 7.1 %far_forward.1 = (f32[384,2048]{1,0:T(8,128)}, f32[3,8,2048]{2,1,0:T(8,128)}, f32[2048,384]{1,0:T(8,128)}) custom-call(s32[6]{0:T(128)} %copy-done.76, s32[1]{0:T(128)} %bitcast.10.far_ref, bf16[1152,2048]{1,0:T(8,128)(2,1)} %copy-done.27, bf16[768,1024]{1,0:T(8,128)(2,1)} %collective-permute-done.16.kx_ref.vx_ref, ...), custom_call_target="tpu_custom_call" | custom-call | flops 6442450944 | bytes 12582912 | tf_op jit(solution)/shard_map/far_forward/pallas_call | solution.py:376
  152.6 6.4 %collective-permute-start.24 = (bf16[4,192,384]{2,1,0:T(8,128)(2,1)}, bf16[4,192,384]{2,1,0:T(8,128)(2,1)}, u32[]{:S(2)}, u32[]{:S(2)}) collective-permute-start(bf16[4,192,384]{2,1,0:T(8,128)(2,1)} %bitcast_dynamic-update-slice_fusion.15), channel_id=1, source_target_pairs={{0,4},{2,6},{4,0},{6,2},{1,5},{3,7},{5,1},{7,3},{8,12},{10,14},{12... | collective-permute-start | bytes 1769480 | tf_op jit(solution)/shard_map/ppermute | solution.py:511
  166.8 7.4 %collective-permute-start.26 = (bf16[4,192,384]{2,1,0:T(8,128)(2,1)}, bf16[4,192,384]{2,1,0:T(8,128)(2,1)}, u32[]{:S(2)}, u32[]{:S(2)}) collective-permute-start(bf16[4,192,384]{2,1,0:T(8,128)(2,1)} %bitcast_dynamic-update-slice_fusion.15), channel_id=1, source_target_pairs={{0,6},{2,4},{4,2},{6,0},{1,7},{3,5},{5,3},{7,1},{8,14},{10,12},{12... | collective-permute-start | bytes 1769480 | tf_op jit(solution)/shard_map/ppermute | solution.py:511
  178.0 3.7 copy.190
  191.7 8.4 %broadcast_add_fusion = f32[1024,3072]{1,0:T(8,128)} fusion(f32[3072]{0:T(1024)S(1)} %copy-done.63, bf16[768,1536]{1,0:T(8,128)(2,1)S(1)} %get-tuple-element.224, bf16[768,1536]{1,0:T(8,128)(2,1)S(1)} %get-tuple-element.223, f32[1024,768]{1,0:T(8,128)S(1)} %get-tuple-element.303, f32[768]{0:T(1024)S(1)} %copy-done.57, f32[1024]{0:T(1024)S(1)} %add_rsqrt_fusion.2, ...), kind=kOutput, calls=%fused_computation.20 | convolution fusion | flops 4847566848 | bytes 20470784 | tf_op jit(solution)/shard_map/dot_general | solution.py:760
  208.1 7.2 %fusion.121 = (f32[1024]{0:T(1024)S(1)}, f32[1024,3072]{1,0:T(8,128)S(1)}) fusion(f32[1024,3072]{1,0:T(8,128)} %broadcast_add_fusion), kind=kLoop, calls=%fused_computation.345 | loop fusion | flops 15727616 | bytes 25169920 | tf_op jit(solution)/shard_map/reduce_sum | solution.py:469
  222.7 15.6 %multiply_reduce_fusion = (bf16[3072]{0:T(1024)(128)(2,1)}, f32[1024]{0:T(1024)S(1)}, f32[1024]{0:T(1024)S(1)}, bf16[1024,3072]{1,0:T(8,128)(2,1)}, f32[1024,3072]{1,0:T(8,128)}) fusion(f32[1024,3072]{1,0:T(8,128)} %copy-done, f32[1024]{0:T(1024)S(1)} %add_rsqrt_fusion.1, f32[1024]{0:T(1024)S(1)} %broadcast_multiply_fusion.4, f32[3072]{0:T(1024)S(1)} %mul.321, ...), kind=kOutput, calls=%fused_computation.7 | convolution fusion | flops 4872727552 | bytes 37783552 | tf_op jit(solution)/shard_map/dot_general | solution.py:777
  238.3 15.0 %fusion.117 = (bf16[3072]{0:T(1024)(128)(2,1)}, bf16[1024,3072]{1,0:T(8,128)(2,1)S(1)}) fusion(f32[1024,3072]{1,0:T(8,128)} %broadcast_add_fusion, f32[1024]{0:T(1024)S(1)} %get-tuple-element.307, f32[1024]{0:T(1024)S(1)} %add_rsqrt_fusion.1, f32[1024,3072]{1,0:T(8,128)} %copy-done, f32[1024]{0:T(1024)S(1)} %broadcast_multiply_fusion.4, ...), kind=kLoop, calls=%fused_computation.343 | loop fusion | flops 56620032 | bytes 44075008 | tf_op jit(solution)/shard_map/reduce_sum | solution.py:784
  253.3 6.2 %multiply_reduce_fusion.5 = (bf16[768]{0:T(1024)(128)(2,1)}, f32[1024]{0:T(1024)S(1)}, f32[1024]{0:T(1024)S(1)}, f32[1024,768]{1,0:T(8,128)S(1)}) fusion(f32[1024,768]{1,0:T(8,128)S(1)} %copy-done.6, f32[1024]{0:T(1024)S(1)} %copy-done.61, f32[1024]{0:T(1024)S(1)} %broadcast_multiply_fusion.11, f32[768]{0:T(1024)S(1)} %copy-done.58, ...), kind=kOutput, calls=%fused_computation.54 | convolution fusion | flops 4847563776 | bytes 17322496 | tf_op jit(solution)/shard_map/dot_general | solution.py:777
  259.4 6.2 %convolution_convert_fusion = bf16[768,3072]{1,0:T(8,128)(2,1)S(1)} fusion(bf16[1024,3072]{1,0:T(8,128)(2,1)S(1)} %get-tuple-element.209, f32[1024,768]{1,0:T(8,128)S(1)} %copy-done.6, f32[768]{0:T(1024)S(1)} %copy-done.58, f32[1024]{0:T(1024)S(1)} %copy-done.61, f32[1024]{0:T(1024)S(1)} %broadcast_multiply_fusion.11), kind=kOutput, calls=%fused_computation.24 | convolution fusion | flops 4837343232 | bytes 14167040 | tf_op jit(solution)/shard_map/dot_general | solution.py:774
  265.7 8.5 %convolution_convert_fusion.1 = bf16[3072,768]{1,0:T(8,128)(2,1)S(1)} fusion(bf16[1024,3072]{1,0:T(8,128)(2,1)} %get-tuple-element.222, bf16[1024,768]{1,0:T(8,128)(2,1)S(1)} %bitcast.429), kind=kOutput, calls=%fused_computation.25 | convolution fusion | flops 4834197504 | bytes 12582912 | tf_op jit(solution)/shard_map/dot_general | solution.py:774
  274.2 9.8 %add_convert_fusion.3 = bf16[1024,768]{1,0:T(8,128)(2,1)} fusion(f32[1024,768]{1,0:T(8,128)S(1)} %copy-done.6, f32[768]{0:T(1024)S(1)} %copy-done.71, bf16[1024,3072]{1,0:T(8,128)(2,1)} %get-tuple-element.222, bf16[3072,384]{1,0:T(8,128)(2,1)S(1)} %get-tuple-element.230, bf16[3072,384]{1,0:T(8,128)(2,1)S(1)} %get-tuple-element.229), kind=kOutput, calls=%fused_computation.62 | convolution fusion | flops 4843634688 | bytes 15731712 | tf_op jit(solution)/shard_map/dot_general | solution.py:770
  295.9 3.7 pad_maximum_fusion.7
  316.7 4.9 collective-permute-done.28
  339.6 5.6 %far_backward.1 = (f32[384,1024]{1,0:T(8,128)}, bf16[2,1024,384]{2,1,0:T(8,128)(2,1)}) custom-call(s32[6]{0:T(128)} %copy-done.76, s32[1]{0:T(128)} %bitcast.10.far_ref, bf16[1152,2048]{1,0:T(8,128)(2,1)} %copy-done.27, bf16[768,1024]{1,0:T(8,128)(2,1)} %collective-permute-done.16.kx_ref.vx_ref, bf16[768,1024]{1,0:T(8,128)(2,1)} %collective-permute-done.16.kx_ref.vx_ref, ...), custom_call_target="tpu_custom_call" | custom-call | flops 16106127360 | bytes 10485760 | tf_op jit(solution)/shard_map/far_backward/pallas_call | solution.py:402
  350.1 12.0 %collective-permute-done.34 = bf16[4,192,384]{2,1,0:T(8,128)(2,1)} collective-permute-done((bf16[4,192,384]{2,1,0:T(8,128)(2,1)}, bf16[4,192,384]{2,1,0:T(8,128)(2,1)}, u32[]{:S(2)}, u32[]{:S(2)}) %collective-permute-start.34) | collective-permute-done | bytes 589856 | tf_op jit(solution)/shard_map/ppermute | solution.py:511
  367.9 4.3 collective-permute-done.36
  372.6 4.1 collective-permute-done.37
  377.9 60.3 %near_backward.1 = (bf16[2048,384]{1,0:T(8,128)(2,1)}, bf16[2,2048,384]{2,1,0:T(8,128)(2,1)}) custom-call(s32[6]{0:T(128)} %copy-done.76, s32[1,2048]{1,0:T(1,128)} %fusion.90.lim_ref, bf16[1152,2048]{1,0:T(8,128)(2,1)} %copy-done.27, bf16[1152,2048]{1,0:T(8,128)(2,1)} %copy-done.27, bf16[1152,2048]{1,0:T(8,128)(2,1)} %copy-done.27, ...), custom_call_target="tpu_custom_call" | custom-call | flops 48318382080 | bytes 14680064 | tf_op jit(solution)/shard_map/near_backward/pallas_call | solution.py:436
  479.3 12.1 %collective-permute-done.52 = bf16[48,1920]{1,0:T(8,128)(2,1)S(1)} collective-permute-done((bf16[48,1920]{1,0:T(8,128)(2,1)S(1)}, bf16[48,1920]{1,0:T(8,128)(2,1)S(1)}, u32[]{:S(2)}, u32[]{:S(2)}) %collective-permute-start.52) | collective-permute-done | bytes 184352 | tf_op jit(solution)/shard_map/ppermute | solution.py:506
  494.5 3.6 fusion.22
  508.2 4.0 fusion.21
  512.4 5.2 collective-permute-done.46
  517.6 8.9 %collective-permute-done.45 = bf16[4,48,1280]{2,1,0:T(8,128)(2,1)S(1)} collective-permute-done((bf16[4,48,1280]{2,1,0:T(8,128)(2,1)S(1)}, bf16[4,48,1280]{2,1,0:T(8,128)(2,1)S(1)}, u32[]{:S(2)}, u32[]{:S(2)}) %collective-permute-start.45) | collective-permute-done | bytes 491552 | tf_op jit(solution)/shard_map/ppermute | solution.py:511
  534.0 6.1 %collective-permute-done.48 = bf16[48,1280]{1,0:T(8,128)(2,1)S(1)} collective-permute-done((bf16[48,1280]{1,0:T(8,128)(2,1)S(1)}, bf16[48,1280]{1,0:T(8,128)(2,1)S(1)}, u32[]{:S(2)}, u32[]{:S(2)}) %collective-permute-start.48) | collective-permute-done | bytes 122912 | tf_op jit(solution)/shard_map/ppermute | solution.py:506
  (488 shorter events, 252.3 us)
Async XLA Ops:
  2.4 24.2 %collective-permute-start.1 = (bf16[24,1920]{1,0:T(8,128)(2,1)S(1)}, bf16[24,1920]{1,0:T(8,128)(2,1)S(1)}, u32[]{:S(2)}, u32[]{:S(2)}) collective-permute-start(bf16[24,1920]{1,0:T(8,128)(2,1)S(1)} %pad_maximum_fusion.20), channel_id=1, source_target_pairs={{0,1},{1,0},{2,3},{3,2},{4,5},{5,4},{6,7},{7,6},{8,9},{9,8},{10,11... | collective-permute-start | bytes 276488 | tf_op jit(solution)/shard_map/ppermute | solution.py:490
  3.8 18.2 %collective-permute-start.5 = (bf16[96,384]{1,0:T(8,128)(2,1)S(1)}, bf16[96,384]{1,0:T(8,128)(2,1)S(1)}, u32[]{:S(2)}, u32[]{:S(2)}) collective-permute-start(bf16[96,384]{1,0:T(8,128)(2,1)S(1)} %constant_dynamic-slice_fusion.13), channel_id=1, source_target_pairs={{0,1},{1,0},{2,3},{3,2},{4,5},{5,4},{6,7},{7,6},{8,9},{9,8},{10,11... | collective-permute-start | bytes 221192 | tf_op jit(solution)/shard_map/ppermute | solution.py:490
  13.4 38.0 %collective-permute-start = (bf16[512,768]{1,0:T(8,128)(2,1)S(1)}, bf16[512,768]{1,0:T(8,128)(2,1)S(1)}, u32[]{:S(2)}, u32[]{:S(2)}) collective-permute-start(bf16[512,768]{1,0:T(8,128)(2,1)S(1)} %dynamic-slice_bitcast_fusion.3), channel_id=1, source_target_pairs={{0,2},{2,0},{1,3},{3,1},{4,6},{6,4},{5,7},{7,5},{8,10},{10,8},{9,1... | collective-permute-start | bytes 2359304 | tf_op jit(solution)/shard_map/ppermute | solution.py:490
  45.4 22.5 %collective-permute-start.12 = (bf16[4,48,1280]{2,1,0:T(8,128)(2,1)S(1)}, bf16[4,48,1280]{2,1,0:T(8,128)(2,1)S(1)}, u32[]{:S(2)}, u32[]{:S(2)}) collective-permute-start(bf16[4,48,1280]{2,1,0:T(8,128)(2,1)S(1)} %bitcast_dynamic-update-slice_fusion.19), channel_id=1, source_target_pairs={{0,6},{2,4},{4,2},{6,0},{1,7},{3,5},{5,3},{7,1},{8,14},{10,12},{12... | collective-permute-start | bytes 1474568 | tf_op jit(solution)/shard_map/ppermute | solution.py:511
  46.9 32.6 %collective-permute-start.14 = (bf16[2,2,48,1920]{3,2,1,0:T(8,128)(2,1)S(1)}, bf16[2,2,48,1920]{3,2,1,0:T(8,128)(2,1)S(1)}, u32[]{:S(2)}, u32[]{:S(2)}) collective-permute-start(bf16[2,2,48,1920]{3,2,1,0:T(8,128)(2,1)S(1)} %bitcast_dynamic-update-slice_fusion.12), channel_id=1, source_target_pairs={{0,8},{8,16},{16,24},{24,0},{1,9},{9,17},{17,25},{25,1},{2,10},{10... | collective-permute-start | bytes 2211848 | tf_op jit(solution)/shard_map/ppermute | solution.py:506
  51.4 34.5 %collective-permute-start.15 = (bf16[2,2,48,1920]{3,2,1,0:T(8,128)(2,1)S(1)}, bf16[2,2,48,1920]{3,2,1,0:T(8,128)(2,1)S(1)}, u32[]{:S(2)}, u32[]{:S(2)}) collective-permute-start(bf16[2,2,48,1920]{3,2,1,0:T(8,128)(2,1)S(1)} %bitcast_dynamic-update-slice_fusion.12), channel_id=1, source_target_pairs={{0,24},{8,0},{16,8},{24,16},{1,25},{9,1},{17,9},{25,17},{2,26},{10... | collective-permute-start | bytes 2211848 | tf_op jit(solution)/shard_map/ppermute | solution.py:506
  57.8 73.2 %collective-permute-start.17 = (bf16[192,384]{1,0:T(8,128)(2,1)}, bf16[192,384]{1,0:T(8,128)(2,1)}, u32[]{:S(2)}, u32[]{:S(2)}) collective-permute-start(bf16[192,384]{1,0:T(8,128)(2,1)} %bitcast.20), channel_id=1, source_target_pairs={{0,8},{8,16},{16,24},{24,0},{1,9},{9,17},{17,25},{25,1},{2,10},{10... | collective-permute-start | bytes 442376 | tf_op jit(solution)/shard_map/ppermute | solution.py:506
  67.9 63.1 %collective-permute-start.18 = (bf16[192,384]{1,0:T(8,128)(2,1)}, bf16[192,384]{1,0:T(8,128)(2,1)}, u32[]{:S(2)}, u32[]{:S(2)}) collective-permute-start(bf16[192,384]{1,0:T(8,128)(2,1)} %bitcast.20), channel_id=1, source_target_pairs={{0,16},{8,24},{16,0},{24,8},{1,17},{9,25},{17,1},{25,9},{2,18},{10... | collective-permute-start | bytes 442376 | tf_op jit(solution)/shard_map/ppermute | solution.py:506
  71.7 59.3 %collective-permute-start.19 = (bf16[192,384]{1,0:T(8,128)(2,1)}, bf16[192,384]{1,0:T(8,128)(2,1)}, u32[]{:S(2)}, u32[]{:S(2)}) collective-permute-start(bf16[192,384]{1,0:T(8,128)(2,1)} %bitcast.20), channel_id=1, source_target_pairs={{0,24},{8,0},{16,8},{24,16},{1,25},{9,1},{17,9},{25,17},{2,26},{10... | collective-permute-start | bytes 442376 | tf_op jit(solution)/shard_map/ppermute | solution.py:506
  79.4 51.6 %collective-permute-start.20 = (bf16[2,2,48,1920]{3,2,1,0:T(8,128)(2,1)S(1)}, bf16[2,2,48,1920]{3,2,1,0:T(8,128)(2,1)}, u32[]{:S(2)}, u32[]{:S(2)}) collective-permute-start(bf16[2,2,48,1920]{3,2,1,0:T(8,128)(2,1)S(1)} %bitcast_dynamic-update-slice_fusion.12), channel_id=1, source_target_pairs={{0,16},{8,24},{16,0},{24,8},{1,17},{9,25},{17,1},{25,9},{2,18},{10... | collective-permute-start | bytes 2211848 | tf_op jit(solution)/shard_map/ppermute | solution.py:506
  98.4 33.9 %collective-permute-start.16 = (bf16[768,1024]{1,0:T(8,128)(2,1)}, bf16[768,1024]{1,0:T(8,128)(2,1)}, u32[]{:S(2)}, u32[]{:S(2)}) collective-permute-start(bf16[768,1024]{1,0:T(8,128)(2,1)} %slice_select_fusion), channel_id=1, source_target_pairs={{0,4},{1,5},{2,6},{3,7},{8,12},{9,13},{10,14},{11,15},{16,20},{17,... | collective-permute-start | bytes 4718600 | tf_op jit(solution)/shard_map/ppermute | solution.py:726
  141.7 33.7 %collective-permute-start.21 = (f32[1024,384]{1,0:T(8,128)S(1)}, f32[1024,384]{1,0:T(8,128)S(1)}, u32[]{:S(2)}, u32[]{:S(2)}) collective-permute-start(f32[1024,384]{1,0:T(8,128)S(1)} %bitcast.448), channel_id=1, source_target_pairs={{0,1},{1,0},{2,3},{3,2},{4,5},{5,4},{6,7},{7,6},{8,9},{9,8},{10,11... | collective-permute-start | bytes 4718600 | tf_op jit(solution)/shard_map/ppermute | solution.py:490
  145.8 38.3 %collective-permute-start.22 = (bf16[768,1920]{1,0:T(8,128)(2,1)}, bf16[768,1920]{1,0:T(8,128)(2,1)}, u32[]{:S(2)}, u32[]{:S(2)}) collective-permute-start(bf16[768,1920]{1,0:T(8,128)(2,1)} %bitcast.58), channel_id=1, source_target_pairs={{0,1},{1,0},{2,3},{3,2},{4,5},{5,4},{6,7},{7,6},{8,9},{9,8},{10,11... | collective-permute-start | bytes 8847368 | tf_op jit(solution)/shard_map/ppermute | solution.py:490
  146.4 20.5 %collective-permute-start.23 = (bf16[512,768]{1,0:T(8,128)(2,1)S(1)}, bf16[512,768]{1,0:T(8,128)(2,1)S(1)}, u32[]{:S(2)}, u32[]{:S(2)}) collective-permute-start(bf16[512,768]{1,0:T(8,128)(2,1)S(1)} %dynamic-slice_bitcast_fusion.2), channel_id=1, source_target_pairs={{0,2},{2,0},{1,3},{3,1},{4,6},{6,4},{5,7},{7,5},{8,10},{10,8},{9,1... | collective-permute-start | bytes 2359304 | tf_op jit(solution)/shard_map/ppermute | solution.py:490
  152.6 47.5 %collective-permute-start.24 = (bf16[4,192,384]{2,1,0:T(8,128)(2,1)}, bf16[4,192,384]{2,1,0:T(8,128)(2,1)}, u32[]{:S(2)}, u32[]{:S(2)}) collective-permute-start(bf16[4,192,384]{2,1,0:T(8,128)(2,1)} %bitcast_dynamic-update-slice_fusion.15), channel_id=1, source_target_pairs={{0,4},{2,6},{4,0},{6,2},{1,5},{3,7},{5,1},{7,3},{8,12},{10,14},{12... | collective-permute-start | bytes 1769480 | tf_op jit(solution)/shard_map/ppermute | solution.py:511
  159.1 41.1 %collective-permute-start.25 = (bf16[4,192,384]{2,1,0:T(8,128)(2,1)}, bf16[4,192,384]{2,1,0:T(8,128)(2,1)}, u32[]{:S(2)}, u32[]{:S(2)}) collective-permute-start(bf16[4,192,384]{2,1,0:T(8,128)(2,1)} %bitcast_dynamic-update-slice_fusion.15), channel_id=1, source_target_pairs={{0,2},{2,0},{4,6},{6,4},{1,3},{3,1},{5,7},{7,5},{8,10},{10,8},{12,... | collective-permute-start | bytes 1769480 | tf_op jit(solution)/shard_map/ppermute | solution.py:511
  166.8 33.3 %collective-permute-start.26 = (bf16[4,192,384]{2,1,0:T(8,128)(2,1)}, bf16[4,192,384]{2,1,0:T(8,128)(2,1)}, u32[]{:S(2)}, u32[]{:S(2)}) collective-permute-start(bf16[4,192,384]{2,1,0:T(8,128)(2,1)} %bitcast_dynamic-update-slice_fusion.15), channel_id=1, source_target_pairs={{0,6},{2,4},{4,2},{6,0},{1,7},{3,5},{5,3},{7,1},{8,14},{10,12},{12... | collective-permute-start | bytes 1769480 | tf_op jit(solution)/shard_map/ppermute | solution.py:511
  285.7 39.9 %collective-permute-start.30 = (bf16[3072,384]{1,0:T(8,128)(2,1)}, bf16[3072,384]{1,0:T(8,128)(2,1)}, u32[]{:S(2)}, u32[]{:S(2)}) collective-permute-start(bf16[3072,384]{1,0:T(8,128)(2,1)} %constant_dynamic-slice_fusion.7), channel_id=1, source_target_pairs={{0,1},{1,0},{2,3},{3,2},{4,5},{5,4},{6,7},{7,6},{8,9},{9,8},{10,11... | collective-permute-start | bytes 7077896 | tf_op jit(solution)/shard_map/ppermute | solution.py:490
  299.8 29.0 %collective-permute-start.31 = (bf16[768,1920]{1,0:T(8,128)(2,1)}, bf16[768,1920]{1,0:T(8,128)(2,1)}, u32[]{:S(2)}, u32[]{:S(2)}) collective-permute-start(bf16[768,1920]{1,0:T(8,128)(2,1)} %pad_maximum_fusion.7), channel_id=1, source_target_pairs={{0,1},{1,0},{2,3},{3,2},{4,5},{5,4},{6,7},{7,6},{8,9},{9,8},{10,11... | collective-permute-start | bytes 8847368 | tf_op jit(solution)/shard_map/ppermute | solution.py:490
  301.8 19.8 %collective-permute-start.28 = (bf16[512,768]{1,0:T(8,128)(2,1)}, bf16[512,768]{1,0:T(8,128)(2,1)}, u32[]{:S(2)}, u32[]{:S(2)}) collective-permute-start(bf16[512,768]{1,0:T(8,128)(2,1)} %dynamic-slice_bitcast_fusion.1), channel_id=1, source_target_pairs={{0,2},{2,0},{1,3},{3,1},{4,6},{6,4},{5,7},{7,5},{8,10},{10,8},{9,1... | collective-permute-start | bytes 2359304 | tf_op jit(solution)/shard_map/ppermute | solution.py:490
  307.4 24.8 %collective-permute-start.29 = (bf16[1024,384]{1,0:T(8,128)(2,1)}, bf16[1024,384]{1,0:T(8,128)(2,1)}, u32[]{:S(2)}, u32[]{:S(2)}) collective-permute-start(bf16[1024,384]{1,0:T(8,128)(2,1)} %bitcast.453), channel_id=1, source_target_pairs={{0,1},{1,0},{2,3},{3,2},{4,5},{5,4},{6,7},{7,6},{8,9},{9,8},{10,11... | collective-permute-start | bytes 2359304 | tf_op jit(solution)/shard_map/ppermute | solution.py:490
  334.1 28.1 %collective-permute-start.34 = (bf16[4,192,384]{2,1,0:T(8,128)(2,1)}, bf16[4,192,384]{2,1,0:T(8,128)(2,1)}, u32[]{:S(2)}, u32[]{:S(2)}) collective-permute-start(bf16[4,192,384]{2,1,0:T(8,128)(2,1)} %get-tuple-element.246), channel_id=1, source_target_pairs={{0,6},{2,4},{4,2},{6,0},{1,7},{3,5},{5,3},{7,1},{8,14},{10,12},{12... | collective-permute-start | bytes 1769480 | tf_op jit(solution)/shard_map/ppermute | solution.py:511
  345.2 93.0 %collective-permute-start.35 = (bf16[2,1024,384]{2,1,0:T(8,128)(2,1)}, bf16[2,1024,384]{2,1,0:T(8,128)(2,1)}, u32[]{:S(2)}, u32[]{:S(2)}) collective-permute-start(bf16[2,1024,384]{2,1,0:T(8,128)(2,1)} %get-tuple-element.94), channel_id=1, source_target_pairs={{4,0},{5,1},{6,2},{7,3},{12,8},{13,9},{14,10},{15,11},{20,16},{21,... | collective-permute-start | bytes 4718600 | tf_op jit(solution)/shard_map/ppermute | solution.py:818
  367.5 70.7 %collective-permute-start.39 = (bf16[4,48,1920]{2,1,0:T(8,128)(2,1)}, bf16[4,48,1920]{2,1,0:T(8,128)(2,1)}, u32[]{:S(2)}, u32[]{:S(2)}) collective-permute-start(bf16[4,48,1920]{2,1,0:T(8,128)(2,1)} %get-tuple-element.243), channel_id=1, source_target_pairs={{0,4},{2,6},{4,0},{6,2},{1,5},{3,7},{5,1},{7,3},{8,12},{10,14},{12... | collective-permute-start | bytes 2211848 | tf_op jit(solution)/shard_map/ppermute | solution.py:511
  367.6 70.6 %collective-permute-start.40 = (bf16[4,48,1920]{2,1,0:T(8,128)(2,1)}, bf16[4,48,1920]{2,1,0:T(8,128)(2,1)}, u32[]{:S(2)}, u32[]{:S(2)}) collective-permute-start(bf16[4,48,1920]{2,1,0:T(8,128)(2,1)} %get-tuple-element.242), channel_id=1, source_target_pairs={{0,2},{2,0},{4,6},{6,4},{1,3},{3,1},{5,7},{7,5},{8,10},{10,8},{12,... | collective-permute-start | bytes 2211848 | tf_op jit(solution)/shard_map/ppermute | solution.py:511
  372.2 66.0 %collective-permute-start.41 = (bf16[4,48,1920]{2,1,0:T(8,128)(2,1)}, bf16[4,48,1920]{2,1,0:T(8,128)(2,1)}, u32[]{:S(2)}, u32[]{:S(2)}) collective-permute-start(bf16[4,48,1920]{2,1,0:T(8,128)(2,1)} %get-tuple-element.241), channel_id=1, source_target_pairs={{0,6},{2,4},{4,2},{6,0},{1,7},{3,5},{5,3},{7,1},{8,14},{10,12},{12... | collective-permute-start | bytes 2211848 | tf_op jit(solution)/shard_map/ppermute | solution.py:511
  376.7 61.5 %collective-permute-start.38 = (bf16[192,384]{1,0:T(8,128)(2,1)S(1)}, bf16[192,384]{1,0:T(8,128)(2,1)S(1)}, u32[]{:S(2)}, u32[]{:S(2)}) collective-permute-start(bf16[192,384]{1,0:T(8,128)(2,1)S(1)} %get-tuple-element.268), channel_id=1, source_target_pairs={{0,24},{8,0},{16,8},{24,16},{1,25},{9,1},{17,9},{25,17},{2,26},{10... | collective-permute-start | bytes 442376 | tf_op jit(solution)/shard_map/ppermute | solution.py:506
  461.5 32.9 %collective-permute-start.42 = (bf16[1024,768]{1,0:T(8,128)(2,1)}, bf16[1024,768]{1,0:T(8,128)(2,1)}, u32[]{:S(2)}, u32[]{:S(2)}) collective-permute-start(bf16[1024,768]{1,0:T(8,128)(2,1)} %bitcast.116), channel_id=1, source_target_pairs={{0,1},{1,0},{2,3},{3,2},{4,5},{5,4},{6,7},{7,6},{8,9},{9,8},{10,11... | collective-permute-start | bytes 4718600 | tf_op jit(solution)/shard_map/ppermute | solution.py:490
  472.3 19.2 %collective-permute-start.52 = (bf16[48,1920]{1,0:T(8,128)(2,1)S(1)}, bf16[48,1920]{1,0:T(8,128)(2,1)S(1)}, u32[]{:S(2)}, u32[]{:S(2)}) collective-permute-start(bf16[48,1920]{1,0:T(8,128)(2,1)S(1)} %get-tuple-element.267), channel_id=1, source_target_pairs={{0,16},{8,24},{16,0},{24,8},{1,17},{9,25},{17,1},{25,9},{2,18},{10... | collective-permute-start | bytes 552968 | tf_op jit(solution)/shard_map/ppermute | solution.py:506
  503.0 23.5 %collective-permute-start.45 = (bf16[4,48,1280]{2,1,0:T(8,128)(2,1)S(1)}, bf16[4,48,1280]{2,1,0:T(8,128)(2,1)S(1)}, u32[]{:S(2)}, u32[]{:S(2)}) collective-permute-start(bf16[4,48,1280]{2,1,0:T(8,128)(2,1)S(1)} %get-tuple-element.257), channel_id=1, source_target_pairs={{0,2},{2,0},{4,6},{6,4},{1,3},{3,1},{5,7},{7,5},{8,10},{10,8},{12,... | collective-permute-start | bytes 1474568 | tf_op jit(solution)/shard_map/ppermute | solution.py:511
  504.7 22.6 %collective-permute-start.44 = (bf16[4,48,1280]{2,1,0:T(8,128)(2,1)S(1)}, bf16[4,48,1280]{2,1,0:T(8,128)(2,1)S(1)}, u32[]{:S(2)}, u32[]{:S(2)}) collective-permute-start(bf16[4,48,1280]{2,1,0:T(8,128)(2,1)S(1)} %get-tuple-element.255), channel_id=1, source_target_pairs={{0,4},{2,6},{4,0},{6,2},{1,5},{3,7},{5,1},{7,3},{8,12},{10,14},{12... | collective-permute-start | bytes 1474568 | tf_op jit(solution)/shard_map/ppermute | solution.py:511
  530.7 18.7 %collective-permute-start.43 = (bf16[512,768]{1,0:T(8,128)(2,1)S(1)}, bf16[512,768]{1,0:T(8,128)(2,1)S(1)}, u32[]{:S(2)}, u32[]{:S(2)}) collective-permute-start(bf16[512,768]{1,0:T(8,128)(2,1)S(1)} %dynamic-slice_bitcast_fusion), channel_id=1, source_target_pairs={{0,2},{2,0},{1,3},{3,1},{4,6},{6,4},{5,7},{7,5},{8,10},{10,8},{9,1... | collective-permute-start | bytes 2359304 | tf_op jit(solution)/shard_map/ppermute | solution.py:490
  (107 other events, 1095.5 us)
